TPU v7x, 32 devices: a whole 2x2x4 slice. The times are simulated.
32 devices in a mesh: dp: 16 (over z, y, x), mp: 2 (over core).
Axes of the slice: x: 2, y: 2, z: 4, core: 2. Of those that a mesh axis runs over, the one named last changes fastest.
Arguments:
- layer_input_rows: bfloat16 [20480, 768], P(('dp', 'mp')), may hold values from -6 to 6
- resolution: int32 [32], P(('dp', 'mp')), may hold values from 0 to 1
- attn_gain: float32 [768], replicated, may hold values from 0.1 to 1.9
- attn_bias: float32 [768], replicated, may hold values from -3 to 3
- qkv_weight: bfloat16 [768, 2304], replicated, may hold values from -0.3125 to 0.3125
- qv_bias: float32 [2, 768], replicated, may hold values from -3 to 3
- out_weight: bfloat16 [768, 768], replicated, may hold values from -0.875 to 0.875
- out_bias: float32 [768], replicated, may hold values from -3 to 3
- attn_scale: float32 [768], replicated, may hold values from 0.5 to 1.5
- ffn_scale: float32 [768], replicated, may hold values from 0.5 to 1.5
- ffn_gain: float32 [2, 768], replicated, may hold values from 0.1 to 1.9
- ffn_bias: float32 [2, 768], replicated, may hold values from -3 to 3
- up_weight: bfloat16 [2, 768, 3072], P(None, 'dp', 'mp'), may hold values from -0.21875 to 0.21875
- up_bias: float32 [2, 3072], P(None, 'mp'), may hold values from -3 to 3
- down_weight: bfloat16 [2, 768, 3072], P(None, 'dp', 'mp'), may hold values from -0.109375 to 0.109375
- down_bias: float32 [2, 768], replicated, may hold values from -3 to 3
- output_gradient: bfloat16 [20480, 768], P(('dp', 'mp')), may hold values from -6 to 6
Outputs:
- block_output: bfloat16 [20480, 768], P(('dp', 'mp'))
- input_grad: bfloat16 [20480, 768], P(('dp', 'mp'))
- attn_gain_grad: float32 [768], replicated
- attn_bias_grad: float32 [768], replicated
- qkv_weight_grad: float32 [768, 2304], P(('dp', 'mp'))
- qv_bias_grad: float32 [2, 768], replicated
- out_weight_grad: float32 [768, 768], P(('dp', 'mp'))
- out_bias_grad: float32 [768], replicated
- attn_scale_grad: float32 [768], replicated
- ffn_scale_grad: float32 [768], replicated
- ffn_gain_grad: float32 [2, 768], replicated
- ffn_bias_grad: float32 [2, 768], replicated
- up_weight_grad: float32 [2, 768, 3072], P(None, 'dp', 'mp')
- up_bias_grad: float32 [2, 3072], replicated
- down_weight_grad: float32 [2, 768, 3072], P(None, 'dp', 'mp')
- down_bias_grad: float32 [2, 768], replicated
All inputs are finite; a program needn't handle non-finite values.
Results may differ from a plain program's by a relative error of at most 0.014.
The roundings to bfloat16 on the way count: a program that leaves them out, or rounds other values in their place, can miss the bound.
Values may be sent and summed in bfloat16 or wider, within the bound.
A program may use at most 256 MiB of HBM per device.

v0:
```python
import jax
import jax.numpy as jnp
from jax import lax
from jax.sharding import PartitionSpec as P

HEADS = 12
PATCH_SMALL = 197
PATCH_LARGE = 577
CAPTION = 40


NORM_EPS = 1e-06
HIGH = lax.Precision.HIGHEST


def layer_norm(field, gain, shift):
    center = field - jnp.mean(field, axis=-1, keepdims=True)
    spread = jnp.mean(center * center, axis=-1, keepdims=True)
    return center * lax.rsqrt(spread + NORM_EPS) * gain + shift


def exact_gelu(field):
    return jax.nn.gelu(field, approximate=False)


def ceil_div(numer, denom):
    return -(-numer // denom)


def slot_layout(res_group, row_count):
    position = jnp.arange(row_count, dtype=jnp.int32)
    small_len = PATCH_SMALL + CAPTION
    large_kind = jnp.where(
        position < PATCH_LARGE, 1, jnp.where(position < PATCH_LARGE + CAPTION, 0, 2)
    )
    large_segment = jnp.where(position < PATCH_LARGE + CAPTION, 0, 2)
    within = position % small_len
    small_kind = jnp.where(position < 2 * small_len, jnp.where(within < PATCH_SMALL, 1, 0), 2)
    small_segment = jnp.where(position < 2 * small_len, position // small_len, 2)
    row_kind = jnp.where(res_group == 1, large_kind, small_kind).astype(jnp.int32)
    segment = jnp.where(res_group == 1, large_segment, small_segment)
    return (row_kind, segment)


def contract_rows(left, right):
    return lax.dot_general(
        left, right, (((0,), (0,)), ((), ())), preferred_element_type=jnp.float32
    )


def contract_cols(left, right):
    return lax.dot_general(
        left, right, (((1,), (1,)), ((), ())), preferred_element_type=jnp.float32
    )


def shards(
    layer_input_rows,
    resolution,
    attn_gain,
    attn_bias,
    qkv_weight,
    qv_bias,
    out_weight,
    out_bias,
    attn_scale,
    ffn_scale,
    ffn_gain,
    ffn_bias,
    up_weight,
    up_bias,
    down_weight,
    down_bias,
    output_gradient,
):
    model_width = layer_input_rows.shape[1]
    slot_count = resolution.shape[0]
    slot_rows = layer_input_rows.shape[0] // slot_count
    head_count = HEADS
    head_width = model_width // head_count
    score_scale = head_width ** (-0.5)
    hidden_part = up_weight.shape[2]
    dp_count = lax.axis_size("dp")
    mp_count = lax.axis_size("mp")
    dp_index = lax.axis_index("dp")
    mp_index = lax.axis_index("mp")
    lang_count = dp_count // 4
    vis_count = dp_count - lang_count
    capacity = max(
        ceil_div(slot_count * PATCH_LARGE, vis_count),
        ceil_div(2 * slot_count * CAPTION, lang_count),
    )
    recv_rows = dp_count * capacity
    kinds, segments = jax.vmap(lambda res_group: slot_layout(res_group, slot_rows))(resolution)
    row_kind = kinds.reshape(-1)
    live_rows = (row_kind != 2).astype(jnp.float32)[:, None]
    vision = (row_kind == 1)[:, None]
    kind_onehot = jnp.stack([row_kind == 0, row_kind == 1], axis=1).astype(jnp.float32)
    rank_vis = jnp.cumsum((row_kind == 1).astype(jnp.int32)) - 1
    rank_txt = jnp.cumsum((row_kind == 0).astype(jnp.int32)) - 1
    target = jnp.where(
        row_kind == 1,
        (rank_vis + dp_index) % vis_count,
        vis_count + (rank_txt + dp_index) % lang_count,
    )
    position = jnp.where(row_kind == 1, rank_vis // vis_count, rank_txt // lang_count)
    slot_index = jnp.where(row_kind == 2, recv_rows, target * capacity + position)

    def to_slots(row_values):
        buffer = (
            jnp.zeros((recv_rows, model_width), row_values.dtype)
            .at[slot_index]
            .set(row_values, mode="drop")
        )
        return buffer.reshape(dp_count, capacity, model_width)

    def from_slots(buffer):
        return jnp.take(
            buffer.reshape(recv_rows, model_width), slot_index, axis=0, mode="fill", fill_value=0
        )

    my_expert = jnp.where(dp_index < vis_count, 1, 0)
    full_up, full_down = (
        lax.all_gather(up_weight, "dp", axis=1, tiled=True),
        lax.all_gather(down_weight, "dp", axis=1, tiled=True),
    )
    own_up = jnp.where(my_expert == 1, full_up[1], full_up[0])
    own_down = jnp.where(my_expert == 1, full_down[1], full_down[0])
    own_up_bias = jnp.where(my_expert == 1, up_bias[1], up_bias[0])
    own_down_bias = jnp.where(my_expert == 1, down_bias[1], down_bias[0])
    x_float = layer_input_rows.astype(jnp.float32)
    normed, norm_pull = jax.vjp(layer_norm, x_float, attn_gain, attn_bias)
    activ = normed.astype(jnp.bfloat16)
    projected = jnp.dot(activ, qkv_weight, preferred_element_type=jnp.float32)
    query = (projected[:, :model_width] + qv_bias[0]).astype(jnp.bfloat16)
    keys = projected[:, model_width : 2 * model_width].astype(jnp.bfloat16)
    values = (projected[:, 2 * model_width :] + qv_bias[1]).astype(jnp.bfloat16)
    query_slots = query.reshape(slot_count, slot_rows, head_count, head_width)
    key_slots = keys.reshape(slot_count, slot_rows, head_count, head_width)
    value_slots = values.reshape(slot_count, slot_rows, head_count, head_width)

    def slot_scores(query_heads, key_heads, segment):
        raw_scores = (
            jnp.einsum("qhd,khd->hqk", query_heads, key_heads, preferred_element_type=jnp.float32)
            * score_scale
        )
        same_seq = (segment[:, None] == segment[None, :])[None]
        return jnp.where(same_seq, raw_scores, -1000000000.0)

    def attend(block_item):
        query_heads, key_heads, value_heads, segment = block_item
        masked = slot_scores(query_heads, key_heads, segment)
        row_max = jnp.max(masked, axis=-1, keepdims=True)
        weights_exp = jnp.exp(masked - row_max)
        row_total = jnp.sum(weights_exp, axis=-1, keepdims=True)
        attn_probs = (weights_exp / row_total).astype(jnp.bfloat16)
        attn_mixed = jnp.einsum(
            "hqk,khd->qhd", attn_probs, value_heads, preferred_element_type=jnp.float32
        )
        log_total = (row_max + jnp.log(row_total))[..., 0]
        return (attn_mixed.reshape(slot_rows, model_width).astype(jnp.bfloat16), log_total)

    attn_mixed, log_totals = lax.map(attend, (query_slots, key_slots, value_slots, segments))
    attn_mixed = attn_mixed.reshape(-1, model_width)
    branch = jnp.dot(attn_mixed, out_weight, preferred_element_type=jnp.float32) + out_bias
    after_attn = x_float + live_rows * attn_scale * branch
    gain_rows = jnp.where(vision, ffn_gain[1], ffn_gain[0])
    shift_rows = jnp.where(vision, ffn_bias[1], ffn_bias[0])
    ffn_normed, norm2_pull = jax.vjp(layer_norm, after_attn, gain_rows, shift_rows)
    sent_rows = ffn_normed.astype(jnp.bfloat16)
    arrived = lax.all_to_all(
        to_slots(sent_rows), "dp", split_axis=0, concat_axis=0, tiled=True
    ).reshape(recv_rows, model_width)
    paired = lax.all_gather(arrived, "mp", axis=0, tiled=True)
    preact = jnp.dot(paired, own_up, preferred_element_type=jnp.float32) + own_up_bias
    hidden, gelu_pull = jax.vjp(exact_gelu, preact)
    hidden_low = hidden.astype(jnp.bfloat16)
    partial_out = contract_cols(hidden_low, own_down)
    expert_sum = (
        lax.psum_scatter(
            partial_out.astype(jnp.bfloat16), "mp", scatter_dimension=0, tiled=True
        ).astype(jnp.float32)
        + own_down_bias
    )
    returned = lax.all_to_all(
        expert_sum.astype(jnp.bfloat16).reshape(dp_count, capacity, model_width),
        "dp",
        split_axis=0,
        concat_axis=0,
        tiled=True,
    )
    expert_rows = from_slots(returned).astype(jnp.float32)
    block_output = (after_attn + live_rows * ffn_scale * expert_rows).astype(jnp.bfloat16)
    grad_float = output_gradient.astype(jnp.float32)
    d_expert = (live_rows * ffn_scale * grad_float).astype(jnp.bfloat16)
    ffn_scale_grad = jnp.sum(live_rows * expert_rows * grad_float, axis=0)
    down_bias_grad = jnp.dot(kind_onehot.T, d_expert.astype(jnp.float32), precision=HIGH)
    arrived_grad = lax.all_to_all(
        to_slots(d_expert), "dp", split_axis=0, concat_axis=0, tiled=True
    ).reshape(recv_rows, model_width)
    paired_grad = lax.all_gather(arrived_grad, "mp", axis=0, tiled=True)
    d_hidden = jnp.dot(paired_grad, own_down, preferred_element_type=jnp.float32)
    d_preact = gelu_pull(d_hidden)[0].astype(jnp.bfloat16)
    own_down_grad = contract_rows(paired_grad, hidden_low)
    own_up_grad = contract_rows(paired, d_preact)
    own_bias_grad = jnp.sum(d_preact.astype(jnp.float32), axis=0)
    d_normed_part = contract_cols(d_preact, own_up)
    d_normed = lax.psum_scatter(
        d_normed_part.astype(jnp.bfloat16), "mp", scatter_dimension=0, tiled=True
    )
    back_grad = lax.all_to_all(
        d_normed.reshape(dp_count, capacity, model_width),
        "dp",
        split_axis=0,
        concat_axis=0,
        tiled=True,
    )
    d_ffn_normed = from_slots(back_grad).astype(jnp.float32)
    d_after_part, gain_grad_rows, shift_grad_rows = norm2_pull(d_ffn_normed)
    ffn_gain_grad = jnp.dot(kind_onehot.T, gain_grad_rows, precision=HIGH)
    ffn_bias_grad = jnp.dot(kind_onehot.T, shift_grad_rows, precision=HIGH)
    d_after = grad_float + d_after_part
    d_branch = (live_rows * attn_scale * d_after).astype(jnp.bfloat16)
    attn_scale_grad = jnp.sum(live_rows * branch * d_after, axis=0)
    out_bias_grad = jnp.sum(d_branch.astype(jnp.float32), axis=0)
    out_weight_grad = contract_rows(attn_mixed, d_branch)
    d_mixed = contract_cols(d_branch, out_weight).astype(jnp.bfloat16)
    d_mixed_slots = d_mixed.reshape(slot_count, slot_rows, head_count, head_width)

    def attend_back(block_item):
        query_heads, key_heads, value_heads, segment, log_total, d_heads = block_item
        masked = slot_scores(query_heads, key_heads, segment)
        probs_full = jnp.exp(masked - log_total[..., None])
        d_probs = jnp.einsum(
            "qhd,khd->hqk", d_heads, value_heads, preferred_element_type=jnp.float32
        )
        row_delta = jnp.sum(probs_full * d_probs, axis=-1, keepdims=True)
        d_scores = (probs_full * (d_probs - row_delta)).astype(jnp.bfloat16)
        probs_low = probs_full.astype(jnp.bfloat16)
        grad_value = jnp.einsum(
            "hqk,qhd->khd", probs_low, d_heads, preferred_element_type=jnp.float32
        )
        grad_query = (
            jnp.einsum("hqk,khd->qhd", d_scores, key_heads, preferred_element_type=jnp.float32)
            * score_scale
        )
        grad_key = (
            jnp.einsum("hqk,qhd->khd", d_scores, query_heads, preferred_element_type=jnp.float32)
            * score_scale
        )
        joined = jnp.concatenate(
            [
                grad_query.reshape(slot_rows, model_width),
                grad_key.reshape(slot_rows, model_width),
                grad_value.reshape(slot_rows, model_width),
            ],
            axis=1,
        )
        return joined.astype(jnp.bfloat16)

    d_projected = lax.map(
        attend_back, (query_slots, key_slots, value_slots, segments, log_totals, d_mixed_slots)
    ).reshape(-1, 3 * model_width)
    qkv_weight_grad = contract_rows(activ, d_projected)
    d_proj_float = d_projected.astype(jnp.float32)
    qv_bias_grad = jnp.stack(
        [
            jnp.sum(d_proj_float[:, :model_width], axis=0),
            jnp.sum(d_proj_float[:, 2 * model_width :], axis=0),
        ]
    )
    d_attn_normed = contract_cols(d_projected, qkv_weight)
    d_input_part, attn_gain_grad, attn_bias_grad = norm_pull(d_attn_normed)
    input_grad = (d_after + d_input_part).astype(jnp.bfloat16)
    expert_pick = (jnp.arange(2) == my_expert).astype(jnp.float32)[:, None, None]
    up_weight_grad, down_weight_grad = (
        lax.psum_scatter(expert_pick * own_up_grad[None], "dp", scatter_dimension=1, tiled=True),
        lax.psum_scatter(expert_pick * own_down_grad[None], "dp", scatter_dimension=1, tiled=True),
    )
    up_bias_full = (
        jnp.zeros((2, mp_count, hidden_part), jnp.float32)
        .at[my_expert, mp_index]
        .set(own_bias_grad)
        .reshape(2, mp_count * hidden_part)
    )
    vector_sums = lax.psum(
        (
            attn_gain_grad,
            attn_bias_grad,
            qv_bias_grad,
            out_bias_grad,
            attn_scale_grad,
            ffn_scale_grad,
            ffn_gain_grad,
            ffn_bias_grad,
            up_bias_full,
            down_bias_grad,
        ),
        ("dp", "mp"),
    )
    matrix_sums = (
        lax.psum_scatter(qkv_weight_grad, ("dp", "mp"), scatter_dimension=0, tiled=True),
        lax.psum_scatter(out_weight_grad, ("dp", "mp"), scatter_dimension=0, tiled=True),
    )
    return (
        block_output,
        input_grad,
        vector_sums[0],
        vector_sums[1],
        matrix_sums[0],
        vector_sums[2],
        matrix_sums[1],
        vector_sums[3],
        vector_sums[4],
        vector_sums[5],
        vector_sums[6],
        vector_sums[7],
        up_weight_grad,
        vector_sums[8],
        down_weight_grad,
        vector_sums[9],
    )


def solution(mesh):
    placed = (
        P(("dp", "mp"), None),
        P(("dp", "mp")),
        P(),
        P(),
        P(),
        P(),
        P(),
        P(),
        P(),
        P(),
        P(),
        P(),
        P(None, "dp", "mp"),
        P(None, "mp"),
        P(None, "dp", "mp"),
        P(),
        P(("dp", "mp"), None),
    )
    return jax.shard_map(
        shards,
        mesh=mesh,
        in_specs=placed,
        out_specs=(
            P(("dp", "mp"), None),
            P(("dp", "mp"), None),
            P(),
            P(),
            P(("dp", "mp"), None),
            P(),
            P(("dp", "mp"), None),
            P(),
            P(),
            P(),
            P(),
            P(),
            P(None, "dp", "mp"),
            P(),
            P(None, "dp", "mp"),
            P(),
        ),
        check_vma=False,
    )
```

profile of v0, /device:TPU:0, one launch (start us, length us, event | category | flops | bytes accessed | tf_op | source)
XLA Modules:
  0.0 1045.2 jit_solution(5351781875264989093)
XLA Ops:
  27.2 3.9 fusion.112
  33.8 2.4 copy.46
  40.7 12.0 %fusion.122 = (f32[12,640]{1,0:T(8,128)}, f32[12,640,640]{1,2,0:T(8,128)}) fusion(bf16[640,12,64]{0,2,1:T(8,128)(2,1)} %bitcast.153, bf16[640,12,64]{0,2,1:T(8,128)(2,1)} %bitcast.151, pred[640,640]{0,1:T(8,128)(4,1)} %broadcast_compare_fusion), kind=kOutput, calls=%fused_computation.254 | convolution fusion | flops 643883520 | bytes 22067200 | tf_op jit(solution)/shard_map/while/body/eval_jaxpr/qhd,khd->hqk/dot_general | solution.py:144
  52.6 9.8 fusion
  62.5 10.5 %fusion.40 = bf16[12,64,640]{2,1,0:T(8,128)(2,1)S(1)} fusion(bf16[640,12,64]{0,2,1:T(8,128)(2,1)} %bitcast.160, f32[12,640,640]{1,2,0:T(8,128)} %get-tuple-element.118, f32[12,640]{1,0:T(8,128)} %fusion, f32[12,640]{1,0:T(8,128)} %get-tuple-element.117), kind=kOutput, calls=%fused_computation.96 | convolution fusion | flops 644382720 | bytes 21688320 | tf_op jit(solution)/shard_map/while/body/eval_jaxpr/hqk,khd->qhd/dot_general | solution.py:157
  73.1 2.5 fusion.121
  79.8 9.8 scatter_custom_fusion
  89.5 2.3 reshape.660
  91.9 42.2 %all_to_all.20 = bf16[16,49,768]{2,1,0:T(8,128)(2,1)} all-to-all(bf16[16,49,768]{2,1,0:T(8,128)(2,1)} %reshape.660), channel_id=1, replica_groups=mesh['dp'=16,'mp'=2] {'dp'}, dimensions={0} | all-to-all | bytes 2408448 | tf_op jit(solution)/shard_map/all_to_all | solution.py:171
  138.0 10.3 scatter_custom_fusion.1
  148.3 2.4 reshape.664
  150.7 4.4 all-to-all-start.2
  156.6 40.2 %all-to-all-done.2 = bf16[16,49,768]{2,1,0:T(8,128)(2,1)} async-done(((bf16[16,49,768]{2,1,0:T(8,128)(2,1)}), bf16[16,49,768]{2,1,0:T(8,128)(2,1)}, u32[]{:S(2)}, u32[]{:S(2)}) %all-to-all-start.2) | async-done | bytes 1204256 | tf_op jit(solution)/shard_map/all_to_all | solution.py:198
  196.7 2.3 reshape.665
  199.2 40.9 %all-gather.7.cloned.1.call-done = bf16[2,768,1536]{2,1,0:T(8,128)(2,1)} async-done(((bf16[2,48,1536]{2,1,0:T(8,128)(2,1)}), bf16[2,768,1536]{2,1,0:T(8,128)(2,1)}) %all-gather.7.cloned.1.call-update) | async-done | bytes 4718608 | tf_op jit(solution)/shard_map/all_gather | solution.py:124
  240.1 28.1 %multiply_convert_fusion.1 = (bf16[1568,1536]{1,0:T(8,128)(2,1)}, f32[1568,1536]{1,0:T(8,128)}, f32[1568,1536]{1,0:T(8,128)}) fusion(f32[1536]{0:T(1024)} %fusion.65, bf16[1568,768]{1,0:T(8,128)(2,1)} %all-gather.5.cloned.1.call-done, bf16[2,768,1536]{2,1,0:T(8,128)(2,1)} %all-gather.7.cloned.1.call-done, pred[]{:T(512)S(6)} %eq.125), kind=kOutput, calls=%fused_computation.19 | convolution fusion | flops 3859513344 | bytes 31217664 | tf_op jit(solution)/shard_map/dot_general | solution.py:175
  268.2 53.0 %all-gather.9.cloned.1.call-done = bf16[2,768,1536]{2,1,0:T(8,128)(2,1)} async-done(((bf16[2,48,1536]{2,1,0:T(8,128)(2,1)}), bf16[2,768,1536]{2,1,0:T(8,128)(2,1)}) %all-gather.9.cloned.1.call-update) | async-done | bytes 4718608 | tf_op jit(solution)/shard_map/all_gather | solution.py:125
  321.2 9.1 convolution_convert_fusion.1
  332.3 13.3 %convert_reduce_fusion = (f32[1536]{0:T(1024)}, bf16[1568,1536]{1,0:T(8,128)(2,1)S(1)}) fusion(f32[1568,1536]{1,0:T(8,128)} %get-tuple-element.105, f32[1568,1536]{1,0:T(8,128)} %get-tuple-element.120, bf16[1568,768]{1,0:T(8,128)(2,1)} %all-gather.11.cloned.1.call-done, bf16[2,768,1536]{2,1,0:T(8,128)(2,1)} %all-gather.9.cloned.1.call-done, pred[]{:T(512)S(6)} %eq.125), kind=kOutput, calls=%fused_computation.17 | convolution fusion | flops 3739089408 | bytes 31217664 | tf_op jit(solution)/shard_map/dot_general | solution.py:202
  347.8 7.6 convolution_convert_fusion
  356.2 2.6 add_convert_fusion.1
  358.7 2.3 reshape.662
  361.1 6.8 all-to-all-start.1
  368.0 2.4 reshape.666
  370.4 28.4 %all-to-all-done.1 = bf16[16,49,768]{2,1,0:T(8,128)(2,1)} async-done(((bf16[16,49,768]{2,1,0:T(8,128)(2,1)}), bf16[16,49,768]{2,1,0:T(8,128)(2,1)}, u32[]{:S(2)}, u32[]{:S(2)}) %all-to-all-start.1) | async-done | bytes 1204256 | tf_op jit(solution)/shard_map/all_to_all | solution.py:185
  398.8 7.5 all-to-all-start.3
  409.2 2.5 reshape.663
  411.7 5.3 gather_fusion
  417.0 19.1 %all-to-all-done.3 = bf16[16,49,768]{2,1,0:T(8,128)(2,1)} async-done(((bf16[16,49,768]{2,1,0:T(8,128)(2,1)}), bf16[16,49,768]{2,1,0:T(8,128)(2,1)}, u32[]{:S(2)}, u32[]{:S(2)}) %all-to-all-start.3) | async-done | bytes 1204256 | tf_op jit(solution)/shard_map/all_to_all | solution.py:211
  436.1 2.4 reshape.667
  438.5 5.5 gather_fusion.1
  444.1 2.7 fusion.25
  446.9 3.5 fusion.119
  454.4 2.5 fusion.123
  459.3 17.7 %multiply_reduce_fusion = (f32[12,640]{1,0:T(8,128)S(1)}, f32[12,640,640]{1,2,0:T(8,128)}) fusion(f32[12,640,640]{1,2,0:T(8,128)} %get-tuple-element.118, f32[12,640]{1,0:T(8,128)} %log_add_fusion, bf16[640,12,64]{0,2,1:T(8,128)(2,1)} %bitcast.155, bf16[640,12,64]{0,2,1:T(8,128)(2,1)} %bitcast.161), kind=kOutput, calls=%fused_computation.5 | convolution fusion | flops 643883520 | bytes 41349120 | tf_op jit(solution)/shard_map/while/body/eval_jaxpr/qhd,khd->hqk/dot_general | solution.py:234
  477.0 14.3 %multiply_convert_fusion = bf16[12,640,640]{1,2,0:T(8,128)(2,1)S(1)} fusion(f32[12,640,640]{1,2,0:T(8,128)} %get-tuple-element.122, f32[12,640,640]{1,2,0:T(8,128)} %get-tuple-element.118, f32[12,640]{1,0:T(8,128)S(1)} %get-tuple-element.121, f32[12,640]{1,0:T(8,128)S(1)} %copy-done.27), kind=kLoop, calls=%fused_computation.4 | loop fusion | flops 19660800 | bytes 49213440 | tf_op jit(solution)/shard_map/while/body/eval_jaxpr/convert_element_type | solution.py:238
  491.3 3.2 multiply_convert_fusion.2
  496.3 10.4 fusion.41
  507.7 6.2 fusion.110
  514.1 7.7 fusion.125
  521.7 6.5 fusion.124
  528.3 7.8 broadcast_multiply_fusion
  550.0 3.4 fusion.117
  558.1 44.6 %all-reduce = (f32[768]{0:T(1024)}, f32[768]{0:T(1024)}, f32[2,768]{1,0:T(2,128)}, f32[768]{0:T(1024)}, f32[768]{0:T(1024)}, /*index=5*/f32[768]{0:T(1024)}, f32...) all-reduce(f32[768]{0:T(1024)} %get-tuple-element.76, ...), channel_id=1, replica_groups=mesh['dp'=16,'mp'=2] {'dp','mp'}, use_global_device_ids=true, to_apply=%region_20.22 | all-reduce | flops 16128 | bytes 129024 | tf_op jit(solution)/shard_map/psum | solution.py:286
  603.4 4.2 add_convert_fusion.2
  607.5 77.2 %reduce-scatter.11.cloned.1.call-done = f32[24,2304]{1,0:T(8,128)} async-done(((f32[768,2304]{1,0:T(8,128)}), f32[24,2304]{1,0:T(8,128)}) %reduce-scatter.11.cloned.1.call-update) | async-done | bytes 221200 | tf_op jit(solution)/shard_map/reduce_scatter | solution.py:302
  684.8 176.6 %reduce-scatter.17.cloned.1.call-done = f32[2,48,1536]{2,1,0:T(8,128)} async-done(((f32[2,768,1536]{2,1,0:T(8,128)}), f32[2,48,1536]{2,1,0:T(8,128)}) %reduce-scatter.17.cloned.1.call-update) | async-done | bytes 589840 | tf_op jit(solution)/shard_map/reduce_scatter | solution.py:278
  861.4 176.6 %reduce-scatter.15.cloned.1.call-done = f32[2,48,1536]{2,1,0:T(8,128)} async-done(((f32[2,768,1536]{2,1,0:T(8,128)}), f32[2,48,1536]{2,1,0:T(8,128)}) %reduce-scatter.15.cloned.1.call-update) | async-done | bytes 589840 | tf_op jit(solution)/shard_map/reduce_scatter | solution.py:277
  (237 shorter events, 71.7 us)
Async XLA Ops:
  7.2 20.0 %copy-start = (bf16[768,2304]{1,0:T(8,128)(2,1)S(1)}, bf16[768,2304]{1,0:T(8,128)(2,1)}, u32[]{:S(2)}) copy-start(bf16[768,2304]{1,0:T(8,128)(2,1)} %param.25) | copy-start | bytes 10616836
  7.2 192.0 %all-gather.5.cloned.1.call-start = ((), (), s32[]{:S(2)}) async-start(), calls=%async_computation.10 | async-start | bytes 3612672 | tf_op jit(solution)/shard_map/all_gather | solution.py:174
  11.3 19.8 %copy-start.35 = (f32[640]{0:T(1024)}, f32[640]{0:T(1024)S(1)}, u32[]{:S(2)}) copy-start(f32[640]{0:T(1024)S(1)} %broadcast_multiply_fusion.3) | copy-start | bytes 7684
  15.2 15.9 %copy-start.34 = (s32[5,128]{1,0:T(8,128)}, s32[5,128]{1,0:T(8,128)S(1)}, u32[]{:S(2)}) copy-start(s32[5,128]{1,0:T(8,128)S(1)} %reduce-window.24) | copy-start | bytes 7684
  16.1 14.9 %copy-start.28 = (s32[5,128]{1,0:T(8,128)}, s32[5,128]{1,0:T(8,128)S(1)}, u32[]{:S(2)}) copy-start(s32[5,128]{1,0:T(8,128)S(1)} %reduce-window.16) | copy-start | bytes 7684
  27.2 5.0 copy-start.62
  27.2 5.0 copy-start.63
  62.5 10.6 %copy-start.4 = (bf16[640,768]{1,0:T(8,128)(2,1)S(1)}, bf16[640,768]{1,0:T(8,128)(2,1)}, u32[]{:S(2)}) copy-start(bf16[640,768]{1,0:T(8,128)(2,1)} %param.21) | copy-start | bytes 2949124
  62.5 10.6 %copy-start.23 = (bf16[768,768]{1,0:T(8,128)(2,1)S(1)}, bf16[768,768]{1,0:T(8,128)(2,1)}, u32[]{:S(2)}) copy-start(bf16[768,768]{1,0:T(8,128)(2,1)} %param.27) | copy-start | bytes 3538948
  62.5 10.6 %copy-start.49 = (f32[768]{0:T(1024)S(1)}, f32[768]{0:T(1024)}, u32[]{:S(2)}) copy-start(f32[768]{0:T(1024)} %param.28) | copy-start | bytes 9220
  62.5 10.6 %copy-start.51 = (f32[768]{0:T(1024)S(1)}, f32[768]{0:T(1024)}, u32[]{:S(2)}) copy-start(f32[768]{0:T(1024)} %param.29) | copy-start | bytes 9220
  73.1 5.4 copy-start.69
  73.1 5.4 copy-start.70
  73.1 6.0 copy-start.57
  73.1 6.0 copy-start.58
  73.1 6.0 copy-start.59
  73.1 6.0 copy-start.72
  79.1 12.8 %copy-start.30 = (f32[768]{0:T(1024)}, f32[768]{0:T(1024)S(1)}, u32[]{:S(2)}) copy-start(f32[768]{0:T(1024)S(1)} %get-tuple-element.133) | copy-start | bytes 9220
  136.5 103.6 %all-gather.7.cloned.1.call-start = ((), (), s32[]{:S(2)}) async-start(), calls=%async_computation.11 | async-start | bytes 5013504 | tf_op jit(solution)/shard_map/all_gather | solution.py:124
  137.2 183.9 %all-gather.9.cloned.1.call-start = ((), (), s32[]{:S(2)}) async-start(), calls=%async_computation.12 | async-start | bytes 5013504 | tf_op jit(solution)/shard_map/all_gather | solution.py:125
  150.7 46.0 %all-to-all-start.2 = ((bf16[16,49,768]{2,1,0:T(8,128)(2,1)}), bf16[16,49,768]{2,1,0:T(8,128)(2,1)}, u32[]{:S(2)}, u32[]{:S(2)}) async-start(bf16[16,49,768]{2,1,0:T(8,128)(2,1)} %reshape.664), calls=%async_computation.3 | async-start | bytes 2752512 | tf_op jit(solution)/shard_map/all_to_all | solution.py:198
  155.1 177.2 %all-gather.11.cloned.1.call-start = ((), (), s32[]{:S(2)}) async-start(), calls=%async_computation.14 | async-start | bytes 3612672 | tf_op jit(solution)/shard_map/all_gather | solution.py:201
  199.1 157.1 %reduce-scatter.7.cloned.1.call-start = ((), (), s32[]{:S(2)}) async-start(), calls=%async_computation.13 | async-start | bytes 3612672 | tf_op jit(solution)/shard_map/reduce_scatter | solution.py:180
  330.3 37.6 %reduce-scatter.9.cloned.1.call-start = ((), (), s32[]{:S(2)}) async-start(), calls=%async_computation.15 | async-start | bytes 3612672 | tf_op jit(solution)/shard_map/reduce_scatter | solution.py:208
  361.1 37.7 %all-to-all-start.1 = ((bf16[16,49,768]{2,1,0:T(8,128)(2,1)}), bf16[16,49,768]{2,1,0:T(8,128)(2,1)}, u32[]{:S(2)}, u32[]{:S(2)}) async-start(bf16[16,49,768]{2,1,0:T(8,128)(2,1)} %reshape.662), calls=%async_computation.2 | async-start | bytes 2752512 | tf_op jit(solution)/shard_map/all_to_all | solution.py:185
  367.9 38.5 %copy-start.29 = (s32[5,128]{1,0:T(8,128)S(1)}, s32[5,128]{1,0:T(8,128)}, u32[]{:S(2)}) copy-start(s32[5,128]{1,0:T(8,128)} %copy-done.28) | copy-start | bytes 7684
  398.8 37.3 %all-to-all-start.3 = ((bf16[16,49,768]{2,1,0:T(8,128)(2,1)}), bf16[16,49,768]{2,1,0:T(8,128)(2,1)}, u32[]{:S(2)}, u32[]{:S(2)}) async-start(bf16[16,49,768]{2,1,0:T(8,128)(2,1)} %reshape.666), calls=%async_computation.5 | async-start | bytes 2752512 | tf_op jit(solution)/shard_map/all_to_all | solution.py:211
  406.3 201.2 %reduce-scatter.13.cloned.1.call-start = ((), (), s32[]{:S(2)}) async-start(), calls=%async_computation.17 | async-start | bytes 2433024 | tf_op jit(solution)/shard_map/reduce_scatter | solution.py:303
  407.8 9.3 copy-start.37
  438.5 5.5 copy-start.31
  459.2 225.6 %reduce-scatter.11.cloned.1.call-start = ((), (), s32[]{:S(2)}) async-start(), calls=%async_computation.16 | async-start | bytes 7299072 | tf_op jit(solution)/shard_map/reduce_scatter | solution.py:302
  459.3 17.7 %copy-start.27 = (f32[12,640]{1,0:T(8,128)S(1)}, f32[12,640]{1,0:T(8,128)}, u32[]{:S(2)}) copy-start(f32[12,640]{1,0:T(8,128)} %log_add_fusion) | copy-start | bytes 92164
  477.0 14.3 %copy-start.12 = (bf16[640,768]{0,1:T(8,128)(2,1)S(1)}, bf16[640,768]{0,1:T(8,128)(2,1)}, u32[]{:S(2)}) copy-start(bf16[640,768]{0,1:T(8,128)(2,1)} %copy.46) | copy-start | bytes 2949124
  494.6 12.2 %copy-start.19 = (bf16[12,64,640]{2,1,0:T(8,128)(2,1)}, bf16[12,64,640]{2,1,0:T(8,128)(2,1)S(1)}, u32[]{:S(2)}) copy-start(bf16[12,64,640]{2,1,0:T(8,128)(2,1)S(1)} %multiply_convert_fusion.2) | copy-start | bytes 2949124
  496.3 10.5 %copy-start.17 = (bf16[12,64,640]{2,1,0:T(8,128)(2,1)}, bf16[12,64,640]{2,1,0:T(8,128)(2,1)S(1)}, u32[]{:S(2)}) copy-start(bf16[12,64,640]{2,1,0:T(8,128)(2,1)S(1)} %multiply_convert_fusion.3) | copy-start | bytes 2949124
  496.3 11.4 %copy-start.5 = (bf16[640,768]{1,0:T(8,128)(2,1)S(1)}, bf16[640,768]{1,0:T(8,128)(2,1)}, u32[]{:S(2)}) copy-start(bf16[640,768]{1,0:T(8,128)(2,1)} %param.21) | copy-start | bytes 2949124
  496.3 11.4 %copy-start.36 = (f32[640]{0:T(1024)S(1)}, f32[640]{0:T(1024)}, u32[]{:S(2)}) copy-start(f32[640]{0:T(1024)} %copy-done.35) | copy-start | bytes 7684
  496.3 11.4 %copy-start.42 = (f32[640]{0:T(1024)S(1)}, f32[640]{0:T(1024)}, u32[]{:S(2)}) copy-start(f32[640]{0:T(1024)} %fusion.96) | copy-start | bytes 7684
  496.3 11.4 %copy-start.60 = (f32[768]{0:T(1024)S(1)}, f32[768]{0:T(1024)}, u32[]{:S(2)}) copy-start(f32[768]{0:T(1024)} %param.23) | copy-start | bytes 9220
  496.3 11.4 %copy-start.74 = (f32[768]{0:T(1024)S(1)}, f32[768]{0:T(1024)}, u32[]{:S(2)}) copy-start(f32[768]{0:T(1024)} %param.24) | copy-start | bytes 9220
  514.0 347.4 %reduce-scatter.17.cloned.1.call-start = ((), (), s32[]{:S(2)}) async-start(), calls=%async_computation.19 | async-start | bytes 10027008 | tf_op jit(solution)/shard_map/reduce_scatter | solution.py:278
  514.1 7.7 copy-start.73
  536.1 501.8 %reduce-scatter.15.cloned.1.call-start = ((), (), s32[]{:S(2)}) async-start(), calls=%async_computation.18 | async-start | bytes 10027008 | tf_op jit(solution)/shard_map/reduce_scatter | solution.py:277
  536.8 5.6 copy-start.64
  536.8 5.6 copy-start.66
  550.0 4.7 copy-start.3
  554.7 48.6 %copy-start.44 = (f32[640]{0:T(1024)S(1)}, f32[640]{0:T(1024)}, u32[]{:S(2)}) copy-start(f32[640]{0:T(1024)} %fusion.96) | copy-start | bytes 7684
  556.5 46.9 %copy-start.46 = (f32[640]{0:T(1024)S(1)}, f32[640]{0:T(1024)}, u32[]{:S(2)}) copy-start(f32[640]{0:T(1024)} %copy-done.45) | copy-start | bytes 7684
  (41 other events, 105.4 us)
Sparse Core Ops, SparseCore 0:
  136.6 8.9 all-gather.4
  148.3 91.7 all-gather.6
  242.8 78.3 all-gather.8
  322.6 9.6 all-gather.10
  334.4 11.3 reduce-scatter.6
  355.5 11.3 reduce-scatter.8
  459.3 100.5 reduce-scatter.12
  566.2 118.5 reduce-scatter.10
  691.1 170.2 reduce-scatter.16
  867.5 170.4 reduce-scatter.14
where the time goes:
time: 1050 us
  waiting for transfers between devices  616 us (59%)
  matrix products  153 us (15%)
  other arithmetic  97.1 us (9%)
  blocking collectives  86.8 us (8%)
  local copies, waits for them, and re-layouts  56.4 us (5%)
  starting transfers between devices  19.2 us (2%)
  between operations  16.3 us (2%)
    reduce_scatter x1, waiting for transfers between devices, shards(): lax.psum_scatter(expert_pick * own_down_grad[None], 'dp', scatter_dimensi...  177 us
    reduce_scatter x1, waiting for transfers between devices, shards(): lax.psum_scatter(expert_pick * own_up_grad[None], 'dp', scatter_dimension...  177 us
    reduce_scatter x1, waiting for transfers between devices, shards(): lax.psum_scatter(qkv_weight_grad, ('dp', 'mp'), scatter_dimension=0, tile...  77.2 us
    all_gather x1, waiting for transfers between devices, shards(): lax.all_gather(down_weight, 'dp', axis=1, tiled=True)  53 us
    psum x1, blocking collectives, shards(): lax.psum((attn_gain_grad, attn_bias_grad, qv_bias_grad, out_bias_grad, at...  44.6 us
    all_to_all x1, blocking collectives, shards(): lax.all_to_all(to_slots(sent_rows), 'dp', split_axis=0, concat_axis=0, ti...  42.2 us
    all_gather x1, waiting for transfers between devices, shards(): lax.all_gather(up_weight, 'dp', axis=1, tiled=True)  40.9 us
    all_to_all x1, waiting for transfers between devices, shards(): lax.all_to_all(to_slots(d_expert), 'dp', split_axis=0, concat_axis=0, til...  40.2 us
  transfers between devices with their start and end apart: 13, of which 9 were waited for; matrix products, arithmetic and copies ran while one was open for 19% of the time, Pallas kernels for 0%

commit v1 on v0

--- a/solution.py
+++ b/solution.py
@@ -1,7 +1,15 @@
+import functools
+
 import jax
 import jax.numpy as jnp
 from jax import lax
+from jax.experimental import pallas as pl
+from jax.experimental.pallas import tpu as pltpu
 from jax.sharding import PartitionSpec as P
+
+MESHID = pl.DeviceIdType.MESH
+BF = jnp.bfloat16
+F32 = jnp.float32
 
 HEADS = 12
 PATCH_SMALL = 197
@@ -322,6 +330,962 @@
     )
 
 
+NT = (((1,), (1,)), ((), ()))
+TN = (((0,), (0,)), ((), ()))
+SMALL = PATCH_SMALL + CAPTION
+CAPS = 2 * CAPTION
+ANY = pl.BlockSpec(memory_space=pl.ANY)
+VM = pl.BlockSpec(memory_space=pltpu.VMEM)
+SM = pl.BlockSpec(memory_space=pltpu.SMEM)
+DMA = pltpu.SemaphoreType.DMA
+CHUNK = 128
+V_AG, V_AB, V_QB, V_VB, V_OB, V_AS, V_FS, V_FG, V_FB, V_DB = 0, 1, 2, 3, 4, 5, 6, 7, 9, 11
+G_AG, G_AB, G_QB, G_VB, G_OB, G_AS, G_FS, G_FG, G_FB, G_DB, G_UB = 0, 1, 2, 3, 4, 5, 6, 7, 9, 11, 16
+
+
+def kind_of(res, pos):
+    one = lambda c: c.astype(jnp.int32)
+    big_seg = 2 * one(pos >= PATCH_LARGE + CAPTION)
+    big_kind = 1 - one(pos >= PATCH_LARGE) + big_seg
+    small_seg = one(pos >= SMALL) + one(pos >= 2 * SMALL)
+    small_pad = one(pos >= 2 * SMALL)
+    within = pos - SMALL * small_seg
+    small_kind = (1 - small_pad) * one(within < PATCH_SMALL) + 2 * small_pad
+    return (
+        res * big_kind + (1 - res) * small_kind,
+        res * big_seg + (1 - res) * small_seg,
+    )
+
+
+def caption_place(res, slot):
+    late = (slot >= CAPTION).astype(jnp.int32)
+    big = (1 - late) * (PATCH_LARGE + slot) - late
+    small = PATCH_SMALL + slot + late * (SMALL - CAPTION)
+    none = (slot >= CAPS).astype(jnp.int32)
+    place = res * big + (1 - res) * small
+    return (1 - none) * place - none
+
+
+def iota(shape, dim):
+    return lax.broadcasted_iota(jnp.int32, shape, dim)
+
+
+def fill_bias(res, bias):
+    n = bias.shape[0]
+    across = kind_of(res, iota((1, n), 1))[1]
+
+    @pl.loop(0, n // CHUNK)
+    def _(r):
+        base = pl.multiple_of(r * CHUNK, CHUNK)
+        down = kind_of(res, iota((CHUNK, 1), 0) + base)[1]
+        bias[pl.ds(base, CHUNK), :] = jnp.where(down == across, 0.0, -1000000000.0)
+
+
+def norm_parts(v):
+    center = v - jnp.mean(v, axis=-1, keepdims=True)
+    inv = lax.rsqrt(jnp.mean(center * center, axis=-1, keepdims=True) + NORM_EPS)
+    return center * inv, inv
+
+
+def norm_back(xhat, inv, d_hat):
+    mean_d = jnp.mean(d_hat, axis=-1, keepdims=True)
+    mean_dx = jnp.mean(d_hat * xhat, axis=-1, keepdims=True)
+    return inv * (d_hat - mean_d - xhat * mean_dx)
+
+
+def half_mask(hh, scale):
+    lane = iota((1, 128), 1)
+    inside = (lane < 64) if hh == 0 else (lane >= 64)
+    return jnp.where(inside, scale, 0.0).astype(BF)
+
+
+def colsum(v):
+    return jnp.sum(v, axis=0, keepdims=True)
+
+
+def dyn_unit(z, k):
+    m = k // 2
+    zz = z + (z // 2) * (3 - 2 * z)
+    u = (1 - m) * (zz + k - 2 * k * zz) + m * k
+    w = z // 2
+    return u + w * (3 - 2 * u)
+
+
+class Place:
+    def __init__(s):
+        s.dp, s.mp = lax.axis_index("dp"), lax.axis_index("mp")
+        s.z = s.dp // 4
+        s.y = (s.dp // 2) % 2
+        s.x = s.dp % 2
+        s.xn = s.dp + 1 - 2 * s.x
+        s.yn = s.dp + 2 - 4 * s.y
+        s.z1 = s.dp + 4 - 8 * (s.z % 2)
+        s.z2 = s.dp + 8 - 16 * (s.z // 2)
+        s.other = 1 - s.mp
+
+    def barrier(s, far=False):
+        bar = pltpu.get_barrier_semaphore()
+        dp, z = s.dp, s.z
+
+        def sig(d, m):
+            pl.semaphore_signal(bar, inc=1, device_id=(d, m), device_id_type=MESHID)
+
+        sig(s.xn, s.mp)
+        sig(s.yn, s.mp)
+        sig(dp, s.other)
+        if far:
+            sig(s.z2, s.mp)
+
+        @pl.when(z > 0)
+        def _():
+            sig(dp - 4, s.mp)
+
+        @pl.when(z < 3)
+        def _():
+            sig(dp + 4, s.mp)
+
+        pl.semaphore_wait(bar, 4 + int(far) + ((z + 1) // 2) % 2)
+
+
+def remote(src, dst, ss, sr, dev, core):
+    return pltpu.make_async_remote_copy(
+        src_ref=src, dst_ref=dst, send_sem=ss, recv_sem=sr,
+        device_id=(dev, core), device_id_type=MESHID,
+    )
+
+
+class AG:
+    def __init__(s, place, g, ss, sr, C):
+        s.p, s.g, s.ss, s.sr, s.C = place, g, ss, sr, C
+        s.rows, s.hid = g.shape[1] // 16, g.shape[2]
+        s.ck = s.hid // C
+        s.col = place.y * 2 + place.x
+
+    def cp(s, kind, c, u, owner, dev, half=None):
+        h = slice(0, 4) if half is None else slice(2 * half, 2 * half + 2)
+        at = pl.ds(pl.multiple_of(owner * s.rows, 16), s.rows)
+        w = s.g.at[h, at, pl.ds(pl.multiple_of(c * s.ck, 128), s.ck)]
+        rk = 0 if kind == 1 else kind
+        return remote(w, w, s.ss.at[kind, c, u], s.sr.at[rk, c, u], dev, s.p.mp)
+
+    def send(s, k, c, local):
+        p = s.p
+        z, dp = p.z, p.dp
+        u = dyn_unit(z, k)
+        owner = u * 4 + s.col
+        if not local:
+            s.cp(0, c, u, owner, dp).wait_recv()
+
+        @pl.when((u <= z) & (z < 3))
+        def _():
+            s.cp(0, c, u, owner, dp + 4).start()
+
+        @pl.when((u >= z) & (z > 0))
+        def _():
+            s.cp(1, c, u, owner, dp - 4).start()
+
+        s.cp(2, c, u, owner, p.xn).start()
+        s.cp(3, c, u, owner, p.yn).start()
+
+    def forward(s, k, c):
+        p = s.p
+        u = dyn_unit(p.z, k)
+        xo = u * 4 + p.y * 2 + 1 - p.x
+        yo = u * 4 + 2 - 2 * p.y + p.x
+        s.cp(2, c, u, xo, p.dp).wait_recv()
+        s.cp(5, c, u, xo, p.yn, half=0).start()
+        s.cp(3, c, u, yo, p.dp).wait_recv()
+        s.cp(4, c, u, yo, p.xn, half=1).start()
+
+    def tick(s, t):
+        c, m = t // 3, t % 3
+        s.send(1 + m, c, False)
+        s.forward(m, c)
+        if isinstance(t, int):
+            if m == 0 and c > 0:
+                s.forward(3, c - 1)
+        else:
+            @pl.when((m == 0) & (c > 0))
+            def _():
+                s.forward(3, c - 1)
+
+    def arrived(s, c):
+        for k in range(4):
+            u = dyn_unit(s.p.z, k)
+            own = u * 4 + s.col
+            s.cp(4, c, u, own, s.p.dp, half=1).wait_recv()
+            s.cp(5, c, u, own, s.p.dp, half=0).wait_recv()
+
+    def finish(s, k, c):
+        p = s.p
+        z, dp = p.z, p.dp
+        u = dyn_unit(z, k)
+        own = u * 4 + s.col
+        s.cp(2, c, u, own, dp).wait_send()
+        s.cp(3, c, u, own, dp).wait_send()
+        s.cp(4, c, u, own, dp, half=1).wait_send()
+        s.cp(5, c, u, own, dp, half=0).wait_send()
+
+        @pl.when((u <= z) & (z < 3))
+        def _():
+            s.cp(0, c, u, own, dp).wait_send()
+
+        @pl.when((u >= z) & (z > 0))
+        def _():
+            s.cp(1, c, u, own, dp).wait_send()
+
+
+class RS:
+    def __init__(s, place, g, bufs, ss, sr, C, write):
+        s.p, s.g, s.write = place, g, write
+        s.bx, s.by, s.bdx, s.bdy, s.bzu, s.bzd = bufs
+        s.ss, s.sr, s.C = ss, sr, C
+        s.M = g.shape[0]
+        s.flat = len(g.shape) == 3
+        s.rows = g.shape[1] // 16 if s.flat else g.shape[2]
+        s.ck = g.shape[-1] // C
+        s.h0 = s.M // 2
+        x, y = place.x, place.y
+        s.oo = y * 2 + x
+        s.ox = y * 2 + 1 - x
+        s.oy = 2 - 2 * y + x
+        s.od = 3 - 2 * y - x
+
+    def cols(s, c):
+        return pl.ds(pl.multiple_of(c * s.ck, 128), s.ck)
+
+    def win(s, u, col, c, lo=0, hi=None):
+        hi = s.M if hi is None else hi
+        if s.flat:
+            at = pl.multiple_of((u * 4 + col) * s.rows, 16)
+            return s.g.at[lo:hi, pl.ds(at, s.rows), s.cols(c)]
+        return s.g.at[lo:hi, u * 4 + col, :, s.cols(c)]
+
+    def cp(s, kind, u, c, src, dst, dev):
+        return remote(src, dst, s.ss.at[kind, c, u], s.sr.at[kind, c, u], dev, s.p.mp)
+
+    def bw(s, b, u, c):
+        return b.at[u, :, :, s.cols(c)]
+
+    def c_dy(s, u, c):
+        return s.cp(0, u, c, s.win(u, s.od, c, 0, s.h0), s.bw(s.bdy, u, c), s.p.yn)
+
+    def c_dx(s, u, c):
+        return s.cp(1, u, c, s.win(u, s.od, c, s.h0), s.bw(s.bdx, u, c), s.p.xn)
+
+    def c_x(s, u, c):
+        return s.cp(2, u, c, s.win(u, s.ox, c), s.bw(s.bx, u, c), s.p.xn)
+
+    def c_y(s, u, c):
+        return s.cp(3, u, c, s.win(u, s.oy, c), s.bw(s.by, u, c), s.p.yn)
+
+    def c_zu(s, u, c):
+        return s.cp(4, u, c, s.win(u, s.oo, c), s.bw(s.bzu, u, c), s.p.dp + 4)
+
+    def c_zd(s, u, c):
+        return s.cp(5, u, c, s.win(u, s.oo, c), s.bw(s.bzd, u, c), s.p.dp - 4)
+
+    def item(s, t):
+        return dyn_unit(s.p.z, 3 - t // s.C), t % s.C
+
+    def s1(s, t):
+        u, c = s.item(t)
+        s.c_dy(u, c).start()
+        s.c_dx(u, c).start()
+
+    def add(s, dst, src):
+        dst[...] = (dst[...].astype(F32) + src[...].astype(F32)).astype(BF)
+
+    def s2(s, t):
+        u, c = s.item(t)
+        s.c_dy(u, c).wait_recv()
+        s.add(s.win(u, s.ox, c, 0, s.h0), s.bw(s.bdy, u, c))
+        s.c_x(u, c).start()
+        s.c_dx(u, c).wait_recv()
+        s.add(s.win(u, s.oy, c, s.h0), s.bw(s.bdx, u, c))
+        s.c_y(u, c).start()
+
+    def s3(s, t):
+        u, c = s.item(t)
+        z = s.p.z
+        s.c_x(u, c).wait_recv()
+        s.c_y(u, c).wait_recv()
+        o = s.win(u, s.oo, c)
+
+        def total(*bufs):
+            v = o[...].astype(F32)
+            for b in (s.bx, s.by) + bufs:
+                v = v + s.bw(b, u, c)[...].astype(F32)
+            return v
+
+        def go(pred, wu, wd, send):
+            @pl.when(pred)
+            def _():
+                more = ()
+                if wu:
+                    s.c_zu(u, c).wait_recv()
+                    more += (s.bzu,)
+                if wd:
+                    s.c_zd(u, c).wait_recv()
+                    more += (s.bzd,)
+                v = total(*more)
+                if send is None:
+                    s.write(c, v)
+                else:
+                    o[...] = v.astype(BF)
+                    send(u, c).start()
+
+        up, dn, own = u > z, u < z, u == z
+        go(up & (z > 0), True, False, s.c_zu)
+        go(up & (z == 0), False, False, s.c_zu)
+        go(dn & (z < 3), False, True, s.c_zd)
+        go(dn & (z == 3), False, False, s.c_zd)
+        go(own & (z == 0), False, True, None)
+        go(own & (z == 3), True, False, None)
+        go(own & (z > 0) & (z < 3), True, True, None)
+
+    def tick(s, t):
+        n = 4 * s.C
+        if t < n:
+            s.s1(t)
+        if 0 <= t - 1 < n:
+            s.s2(t - 1)
+        if 0 <= t - 2 < n:
+            s.s3(t - 2)
+
+    def finish(s, t):
+        u, c = s.item(t)
+        for f in (s.c_dy, s.c_dx, s.c_x, s.c_y):
+            f(u, c).wait_send()
+
+        @pl.when(u > s.p.z)
+        def _():
+            s.c_zu(u, c).wait_send()
+
+        @pl.when(u < s.p.z)
+        def _():
+            s.c_zd(u, c).wait_send()
+
+
+def load_all(pairs, sem):
+    copies = [pltpu.make_async_copy(a, b, sem.at[i]) for i, (a, b) in enumerate(pairs)]
+    for c in copies:
+        c.start()
+    return copies
+
+
+def front_kernel(
+    C, res_ref, a_gain, a_bias, qv_bias, o_bias, a_scale, f_scale, f_gain, f_bias, dn_bias, up_bias,
+    x, og, wqkv, wout, up_ref, down_ref,
+    proj, activ, mixed, vec, ub, fsum, bsum, grads,
+    g, bias, qkvb, xall, gall, xt, gt, xct, gct, accf, accb, rcv, stage, hid, dpre, ubg,
+    lsem, ss, sr, ps, pr,
+):
+    p = Place()
+    n, width = x.shape
+    res = res_ref[0]
+    ag = AG(p, g, ss, sr, C)
+    mine = pl.ds(pl.multiple_of(p.dp * ag.rows, 16), ag.rows)
+    loads = load_all([(up_ref, g.at[0:2, mine, :]), (down_ref, g.at[2:4, mine, :])], lsem)
+    p.barrier()
+    for c in loads:
+        c.wait()
+    for c in range(C):
+        ag.send(0, c, True)
+
+    for row, ref in (
+        (V_AG, a_gain), (V_AB, a_bias), (V_OB, o_bias), (V_AS, a_scale), (V_FS, f_scale),
+    ):
+        vec[row:row + 1, :] = ref[...].reshape(1, width)
+    for row, ref in ((V_QB, qv_bias), (V_FG, f_gain), (V_FB, f_bias), (V_DB, dn_bias)):
+        vec[row:row + 2, :] = ref[...]
+    vec[13:16, :] = jnp.zeros((3, width), F32)
+
+    @pl.loop(0, n // CHUNK)
+    def _(r):
+        at = pl.ds(pl.multiple_of(r * CHUNK, CHUNK), CHUNK)
+        hat, _ = norm_parts(x[at, :].astype(F32))
+        activ[at, :] = (hat * vec[V_AG:V_AG + 1, :] + vec[V_AB:V_AB + 1, :]).astype(BF)
+
+    qkvb[:, :width] = vec[V_QB:V_QB + 1, :]
+    qkvb[:, width:2 * width] = jnp.zeros((1, width), F32)
+    qkvb[:, 2 * width:] = vec[V_VB:V_VB + 1, :]
+    part = 384
+
+    @pl.loop(0, 3 * width // part)
+    def _(j):
+        at = pl.ds(pl.multiple_of(j * part, 128), part)
+        v = jnp.dot(activ[...], wqkv[:, at], preferred_element_type=F32)
+        proj[:, at] = (v + qkvb[:, at]).astype(BF)
+
+    fill_bias(res, bias)
+    masks = [half_mask(0, 0.125), half_mask(1, 0.125)]
+    first = iota((1, 128), 1) < 64
+
+    @pl.loop(0, width // 128)
+    def _(h):
+        def cols(base):
+            return pl.ds(pl.multiple_of(base + h * 128, 128), 128)
+
+        @pl.when(h > 0)
+        def _():
+            ag.tick(h - 1)
+
+        q, k, v = proj[:, cols(0)], proj[:, cols(width)], proj[:, cols(2 * width)]
+        outs = []
+        for hh in range(2):
+            s = lax.dot_general(q * masks[hh], k, NT, preferred_element_type=F32) + bias[...]
+            e = jnp.exp(s - jnp.max(s, axis=-1, keepdims=True))
+            pr_low = (e * (1.0 / jnp.sum(e, axis=-1, keepdims=True))).astype(BF)
+            outs.append(jnp.dot(pr_low, v, preferred_element_type=F32))
+        mixed[:, cols(0)] = jnp.where(first, outs[0], outs[1]).astype(BF)
+
+    ag.tick(5)
+    half = 256
+
+    @pl.loop(0, width // half)
+    def _(j):
+        at = pl.ds(pl.multiple_of(j * half, 128), half)
+        accf[:n, at] = jnp.dot(mixed[...], wout[:, at], preferred_element_type=F32)
+
+    img = p.mp * n
+    caps = 2 * n + p.mp * CAPS
+
+    @pl.loop(0, n // CHUNK)
+    def _(r):
+        base = pl.multiple_of(r * CHUNK, CHUNK)
+        at = pl.ds(base, CHUNK)
+        to = pl.ds(pl.multiple_of(img + base, 128), CHUNK)
+        kind = kind_of(res, iota((CHUNK, 1), 0) + base)[0]
+        live = (kind < 2).astype(F32)
+        row = x[at, :].astype(F32)
+        row = row + live * vec[V_AS:V_AS + 1, :] * (accf[at, :] + vec[V_OB:V_OB + 1, :])
+        hat, _ = norm_parts(row)
+        gain = jnp.where(kind == 1, vec[V_FG + 1:V_FG + 2, :], vec[V_FG:V_FG + 1, :])
+        shift = jnp.where(kind == 1, vec[V_FB + 1:V_FB + 2, :], vec[V_FB:V_FB + 1, :])
+        xall[to, :] = (hat * gain + shift).astype(BF)
+        gall[to, :] = (live * vec[V_FS:V_FS + 1, :] * og[at, :].astype(F32)).astype(BF)
+
+    pick = (iota((CAPS, n), 1) == caption_place(res, iota((CAPS, 1), 0))).astype(F32).astype(BF)
+    at_img = pl.ds(pl.multiple_of(img, 128), n)
+    at_cap = pl.ds(pl.multiple_of(caps, 16), CAPS)
+    for ref in (xall, gall):
+        ref[at_cap, :] = jnp.dot(pick, ref[at_img, :], preferred_element_type=F32).astype(BF)
+
+    @pl.loop(0, n // CHUNK)
+    def _(r):
+        base = pl.multiple_of(r * CHUNK, CHUNK)
+        to = pl.ds(pl.multiple_of(img + base, 128), CHUNK)
+        vis = (kind_of(res, iota((CHUNK, 1), 0) + base)[0] == 1).astype(F32)
+        gall[to, :] = (gall[to, :].astype(F32) * vis).astype(BF)
+
+    pairs = []
+    for i, (ref, at) in enumerate(((xall, at_img), (xall, at_cap), (gall, at_img), (gall, at_cap))):
+        w = ref.at[at, :]
+        pairs.append(remote(w, w, ps.at[i], pr.at[i], p.dp, p.other))
+        pairs[-1].start()
+    ag.tick(6)
+    accf[...] = jnp.zeros(accf.shape, F32)
+    accb[...] = jnp.zeros(accb.shape, F32)
+    ubg[...] = jnp.zeros(ubg.shape, F32)
+    for c in pairs:
+        c.wait()
+    for src, dst in ((xall, xt), (gall, gt)):
+        @pl.loop(0, 2 * n // CHUNK)
+        def _(r):
+            at = pl.ds(pl.multiple_of(r * CHUNK, CHUNK), CHUNK)
+            dst[:, at] = src[at, :].T
+
+    xct[...] = xall[2 * n:, :].T
+    gct[...] = gall[2 * n:, :].T
+    ag.tick(7)
+    ck = ag.ck
+
+    def saved(c):
+        return pltpu.make_async_copy(stage, grads.at[:, :, c * ck:(c + 1) * ck], lsem.at[2])
+
+    def rows_step(c, expert, at):
+        here = slice(c * ck, (c + 1) * ck)
+        up, down = g[expert, :, here], g[2 + expert, :, here]
+        v = jnp.dot(xall[at, :], up, preferred_element_type=F32) + up_bias[expert:expert + 1, here]
+        dh = jnp.dot(gall[at, :], down, preferred_element_type=F32)
+        cdf = 0.5 * (1.0 + lax.erf(v * (0.5 ** 0.5)))
+        slope = cdf + v * (jnp.exp(v * v * -0.5) * 0.3989422804014327)
+        h_low = (v * cdf).astype(BF)
+        d_low = (dh * slope).astype(BF)
+        hid[at, :] = h_low
+        dpre[at, :] = d_low
+        accf[at, :] += lax.dot_general(h_low, down, NT, preferred_element_type=F32)
+        accb[at, :] += lax.dot_general(d_low, up, NT, preferred_element_type=F32)
+        ubg[expert:expert + 1, here] += colsum(d_low.astype(F32))
+
+    back_pairs = []
+    for c in range(C):
+        ag.arrived(c)
+
+        @pl.loop(0, 2 * n // 256)
+        def _(r):
+            rows_step(c, 1, pl.ds(pl.multiple_of(r * 256, 256), 256))
+
+        rows_step(c, 0, slice(2 * n, 2 * n + 2 * CAPS))
+        if c == 0:
+            ag.tick(8)
+        if c == C - 1:
+            theirs_img = pl.ds(pl.multiple_of(p.other * n, 128), n)
+            theirs_cap = pl.ds(pl.multiple_of(2 * n + p.other * CAPS, 16), CAPS)
+            for i, (acc, low) in enumerate(((accf, xall), (accb, gall))):
+                @pl.loop(0, 9)
+                def _(r):
+                    at = pl.ds(pl.multiple_of(r * 160, 16), 160)
+                    low[at, :] = acc[at, :].astype(BF)
+
+                for j, (at, lo, size) in enumerate(((theirs_img, 0, n), (theirs_cap, n, CAPS))):
+                    k = 2 * i + j
+                    to = rcv.at[pl.ds(i * (n + CAPS) + lo, size), :]
+                    back_pairs.append(
+                        remote(low.at[at, :], to, ps.at[4 + k], pr.at[4 + k], p.dp, p.other)
+                    )
+                    back_pairs[-1].start()
+        if c > 0:
+            saved(c - 1).wait()
+
+        @pl.loop(0, width // 256)
+        def _(r):
+            at = pl.ds(pl.multiple_of(r * 256, 256), 256)
+            im = slice(0, 2 * n)
+            cp = slice(2 * n, 2 * n + 2 * CAPS)
+            for i, (l, rr, rows) in enumerate(
+                ((xct, dpre, cp), (xt, dpre, im), (gct, hid, cp), (gt, hid, im))
+            ):
+                stage[i, at, :] = jnp.dot(
+                    l[at, :], rr[rows, :], preferred_element_type=F32
+                ).astype(BF)
+
+        saved(c).start()
+        if c == 0:
+            ag.forward(3, C - 1)
+    ub[...] = jnp.zeros(ub.shape, F32)
+    for e in range(2):
+        for j in range(2):
+            ub[pl.ds(e * 4 + p.mp * 2 + j, 1), :] = ubg[e:e + 1, j * width:(j + 1) * width]
+    for c in back_pairs:
+        c.wait()
+    for i, (low, out) in enumerate(((xall, fsum), (gall, bsum))):
+        off = i * (n + CAPS)
+
+        @pl.loop(0, n // CHUNK)
+        def _(r):
+            base = r * CHUNK
+            at = pl.ds(pl.multiple_of(base, CHUNK), CHUNK)
+            own = low[pl.ds(pl.multiple_of(img + base, CHUNK), CHUNK), :].astype(F32)
+            got = rcv[pl.ds(pl.multiple_of(off + base, 16), CHUNK), :].astype(F32)
+            out[at, :] = (own + got).astype(BF)
+
+        own = low[at_cap, :].astype(F32)
+        out[n:, :] = (own + rcv[off + n:off + n + CAPS, :].astype(F32)).astype(BF)
+    saved(C - 1).wait()
+    for k in range(4):
+        for c in range(C):
+            ag.finish(k, c)
+
+
+def front(res, small, up_bias, x, og, wqkv, wout, up, down, C=3):
+    n, width = x.shape
+    _, rows, hid = up.shape
+    ck = hid // C
+    sds = jax.ShapeDtypeStruct
+    wide = 2 * (n + CAPS)
+    return pl.pallas_call(
+        functools.partial(front_kernel, C),
+        out_shape=(
+            sds((n, 3 * width), BF),
+            sds((n, width), BF),
+            sds((n, width), BF),
+            sds((16, width), F32),
+            sds((8, width), F32),
+            sds((n + CAPS, width), BF),
+            sds((n + CAPS, width), BF),
+            sds((4, rows * 16, hid), BF),
+        ),
+        in_specs=[SM] + [VM] * 14 + [ANY, ANY],
+        out_specs=(VM,) * 7 + (ANY,),
+        scratch_shapes=[
+            pltpu.VMEM((4, rows * 16, hid), BF),
+            pltpu.VMEM((n, n), F32),
+            pltpu.VMEM((1, 3 * width), F32),
+            pltpu.VMEM((wide, width), BF),
+            pltpu.VMEM((wide, width), BF),
+            pltpu.VMEM((width, 2 * n), BF),
+            pltpu.VMEM((width, 2 * n), BF),
+            pltpu.VMEM((width, 2 * CAPS), BF),
+            pltpu.VMEM((width, 2 * CAPS), BF),
+            pltpu.VMEM((wide, width), F32),
+            pltpu.VMEM((wide, width), F32),
+            pltpu.VMEM((wide, width), BF),
+            pltpu.VMEM((4, rows * 16, ck), BF),
+            pltpu.VMEM((wide, ck), BF),
+            pltpu.VMEM((wide, ck), BF),
+            pltpu.VMEM((2, hid), F32),
+            DMA((3,)), DMA((6, C, 4)), DMA((6, C, 4)), DMA((8,)), DMA((8,)),
+        ],
+        compiler_params=pltpu.CompilerParams(
+            collective_id=0, has_side_effects=True, vmem_limit_bytes=67043328
+        ),
+        name="front",
+    )(res, *small, up_bias, x, og, wqkv, wout, up, down)
+
+
+def back_kernel(
+    C, res_ref, vec, ub, x, og, fsum, bsum, proj_h, mixed_h, wout, grads_h,
+    out_up, out_down, block, d_proj, d_branch, d_after, vsum,
+    g, bx, by, bdx, bdy, bzu, bzd, proj, mixed, capf, branch, d_mixed, bias,
+    lsem, ss, sr,
+):
+    p = Place()
+    n, width = x.shape
+    res = res_ref[0]
+    loads = load_all([(grads_h, g), (proj_h, proj), (mixed_h, mixed)], lsem)
+    p.barrier()
+
+    def write(c, v):
+        at = pl.ds(pl.multiple_of(c * (g.shape[2] // C), 128), g.shape[2] // C)
+        out_up[:, :, at] = v[:2]
+        out_down[:, :, at] = v[2:]
+
+    rs = RS(p, g, (bx, by, bdx, bdy, bzu, bzd), ss, sr, C, write)
+    loads[0].wait()
+    rs.tick(0)
+    loads[1].wait()
+    loads[2].wait()
+    fill_bias(res, bias)
+    half = 256
+
+    @pl.loop(0, width // half)
+    def _(j):
+        at = pl.ds(pl.multiple_of(j * half, 128), half)
+        branch[:, at] = jnp.dot(mixed[...], wout[:, at], preferred_element_type=F32)
+
+    vsum[...] = jnp.zeros(vsum.shape, F32)
+    vsum[G_UB:G_UB + 8, :] = ub[...]
+    pad = jnp.zeros((128 - CAPS, width), BF)
+    for i, ref in enumerate((fsum, bsum)):
+        capf[i] = jnp.concatenate([ref[n:, :], pad], axis=0)
+
+    def add(row, v):
+        vsum[row:row + 1, :] += colsum(v)
+
+    @pl.loop(0, n // CHUNK)
+    def _(r):
+        base = pl.multiple_of(r * CHUNK, CHUNK)
+        at = pl.ds(base, CHUNK)
+        pos = iota((CHUNK, 1), 0) + base
+        kind = kind_of(res, pos)[0]
+        live = (kind < 2).astype(F32)
+        vis = kind == 1
+        cap = kind == 0
+        pick = (pos == caption_place(res, iota((1, 128), 1))).astype(F32).astype(BF)
+        from_cap = jnp.dot(pick, capf[0], preferred_element_type=F32)
+        d_cap = jnp.dot(pick, capf[1], preferred_element_type=F32)
+        from_img = fsum[at, :].astype(F32)
+        d_img = bsum[at, :].astype(F32)
+        grad = og[at, :].astype(F32)
+        row_branch = branch[at, :] + vec[V_OB:V_OB + 1, :]
+        scale = live * vec[V_AS:V_AS + 1, :]
+        after = x[at, :].astype(F32) + scale * row_branch
+        expert = jnp.where(
+            cap, from_cap + vec[V_DB:V_DB + 1, :], from_img + vec[V_DB + 1:V_DB + 2, :]
+        ).astype(BF).astype(F32)
+        ffn_scale = live * vec[V_FS:V_FS + 1, :]
+        block[at, :] = (after + ffn_scale * expert).astype(BF)
+        add(G_FS, live * expert * grad)
+        d_expert = (ffn_scale * grad).astype(BF).astype(F32)
+        add(G_DB, jnp.where(cap, d_expert, 0.0))
+        add(G_DB + 1, jnp.where(vis, d_expert, 0.0))
+        d_ffn = jnp.where(cap, d_cap, d_img)
+        hat, inv = norm_parts(after)
+        d_gain = d_ffn * hat
+        add(G_FG, jnp.where(cap, d_gain, 0.0))
+        add(G_FG + 1, jnp.where(vis, d_gain, 0.0))
+        add(G_FB, jnp.where(cap, d_ffn, 0.0))
+        add(G_FB + 1, jnp.where(vis, d_ffn, 0.0))
+        gain = jnp.where(vis, vec[V_FG + 1:V_FG + 2, :], vec[V_FG:V_FG + 1, :])
+        da = grad + norm_back(hat, inv, d_ffn * gain)
+        d_after[at, :] = da
+        add(G_AS, live * row_branch * da)
+        db = (scale * da).astype(BF)
+        d_branch[at, :] = db
+        add(G_OB, db.astype(F32))
+
+    rs.tick(1)
+
+    @pl.loop(0, width // half)
+    def _(j):
+        at = pl.ds(pl.multiple_of(j * half, 128), half)
+        v = lax.dot_general(d_branch[...], wout[at, :], NT, preferred_element_type=F32)
+        d_mixed[:, at] = v.astype(BF)
+
+    ones = [half_mask(0, 1.0), half_mask(1, 1.0)]
+    scaled = [half_mask(0, 0.125), half_mask(1, 0.125)]
+    first = iota((1, 128), 1) < 64
+
+    @pl.loop(0, width // 128)
+    def _(h):
+        t = h + 2
+        rs.s1(t)
+        rs.s2(t - 1)
+        rs.s3(t - 2)
+
+        def cols(base):
+            return pl.ds(pl.multiple_of(base + h * 128, 128), 128)
+
+        q, k, v = proj[:, cols(0)], proj[:, cols(width)], proj[:, cols(2 * width)]
+        do = d_mixed[:, cols(0)]
+        q_scaled = q * jnp.full((1, 128), 0.125, BF)
+        k_turned = (k.astype(F32) * 0.125).T.astype(BF)
+        dq, dk, dv = [], [], []
+        for hh in range(2):
+            s = lax.dot_general(k * scaled[hh], q, NT, preferred_element_type=F32) + bias[...]
+            e = jnp.exp(s - jnp.max(s, axis=0, keepdims=True))
+            pt = e * (1.0 / jnp.sum(e, axis=0, keepdims=True))
+            dpt = lax.dot_general(v * ones[hh], do, NT, preferred_element_type=F32)
+            delta = jnp.sum(pt * dpt, axis=0, keepdims=True)
+            dst = (pt * (dpt - delta)).astype(BF)
+            dv.append(jnp.dot(pt.astype(BF), do, preferred_element_type=F32))
+            dk.append(jnp.dot(dst, q_scaled, preferred_element_type=F32))
+            dq.append(jnp.dot(k_turned[64 * hh:64 * hh + 64], dst, preferred_element_type=F32))
+        dq_all = jnp.concatenate(dq, axis=0).T.astype(BF)
+        dv_all = jnp.where(first, dv[0], dv[1]).astype(BF)
+        d_proj[:, cols(0)] = dq_all
+        d_proj[:, cols(width)] = jnp.where(first, dk[0], dk[1]).astype(BF)
+        d_proj[:, cols(2 * width)] = dv_all
+        vsum[G_QB:G_QB + 1, cols(0)] = colsum(dq_all.astype(F32))
+        vsum[G_VB:G_VB + 1, cols(0)] = colsum(dv_all.astype(F32))
+
+    rs.tick(4 * C)
+    rs.tick(4 * C + 1)
+    for t in range(4 * C):
+        rs.finish(t)
+
+
+def back(res, vec, ub, x, og, fsum, bsum, proj, mixed, wout, grads, C=2):
+    n, width = x.shape
+    M, rows, hid = grads.shape[0], grads.shape[1] // 16, grads.shape[2]
+    sds = jax.ShapeDtypeStruct
+    full = pltpu.VMEM((4, M, rows, hid), BF)
+    part = pltpu.VMEM((4, M // 2, rows, hid), BF)
+    return pl.pallas_call(
+        functools.partial(back_kernel, C),
+        out_shape=(
+            sds((2, rows, hid), F32),
+            sds((2, rows, hid), F32),
+            sds((n, width), BF),
+            sds((n, 3 * width), BF),
+            sds((n, width), BF),
+            sds((n, width), F32),
+            sds((24, width), F32),
+        ),
+        in_specs=[SM] + [VM] * 6 + [ANY, ANY, VM, ANY],
+        out_specs=(VM,) * 7,
+        scratch_shapes=[
+            pltpu.VMEM((M, 16 * rows, hid), BF),
+            full, full, part, part, full, full,
+            pltpu.VMEM((n, 3 * width), BF),
+            pltpu.VMEM((n, width), BF),
+            pltpu.VMEM((2, 128, width), BF),
+            pltpu.VMEM((n, width), F32),
+            pltpu.VMEM((n, width), BF),
+            pltpu.VMEM((n, n), F32),
+            DMA((3,)), DMA((6, C, 4)), DMA((6, C, 4)),
+        ],
+        compiler_params=pltpu.CompilerParams(
+            collective_id=1, has_side_effects=True, vmem_limit_bytes=63 << 20
+        ),
+        name="back",
+    )(res, vec, ub, x, og, fsum, bsum, proj, mixed, wout, grads)
+
+
+def tail_kernel(
+    C, vec, x, activ, mixed, d_proj, d_branch, d_after, wqkv, vin,
+    qkv_out, out_out, d_in, vout,
+    full, split, got, g, bx, by, bdx, bdy, bzu, bzd, dn, vs, vr,
+    ss, sr, ps, pr, vss, vsr,
+):
+    p = Place()
+    n, width = x.shape
+    rows = qkv_out.shape[0]
+    p.barrier(far=True)
+
+    def pair(j):
+        return remote(split.at[p.other, j], got.at[j], ps.at[j], pr.at[j], p.dp, p.other)
+
+    for j in (0, 2, 1, 3):
+        if j < 3:
+            full[...] = lax.dot_general(
+                activ[...], d_proj[:, j * width:(j + 1) * width], TN, preferred_element_type=F32
+            )
+        else:
+            full[...] = lax.dot_general(mixed[...], d_branch[...], TN, preferred_element_type=F32)
+
+        @pl.loop(0, 16)
+        def _(o):
+            for core in range(2):
+                at = pl.ds(pl.multiple_of((2 * o + core) * rows, 8), rows)
+                split[core, j, o] = full[at, :].astype(BF)
+
+        pair(j).start()
+
+    def write(c, v):
+        if True:
+            at = pl.ds(pl.multiple_of(c * width, 128), width)
+            qkv_out[:, at] = v[0]
+
+            @pl.when(c == 0)
+            def _():
+                qkv_out[:, 2 * width:] = v[1]
+
+            @pl.when(c == 1)
+            def _():
+                out_out[...] = v[1]
+
+    rs = RS(p, g, (bx, by, bdx, bdy, bzu, bzd), ss, sr, C, write)
+    for j in (0, 2, 1, 3):
+        pair(j).wait()
+
+        @pl.loop(0, 16)
+        def _(o):
+            v = split[p.mp, j, o].astype(F32) + got[j, o].astype(F32)
+            g[j // 2, o, :, (j % 2) * width:(j % 2 + 1) * width] = v.astype(BF)
+
+    rs.tick(0)
+    rs.tick(1)
+    half = 256
+    vs[0] = vin[...]
+
+    @pl.loop(0, width // half)
+    def _(j):
+        at = pl.ds(pl.multiple_of(j * half, 128), half)
+        dn[:, at] = lax.dot_general(d_proj[...], wqkv[at, :], NT, preferred_element_type=F32)
+
+    rs.tick(2)
+    rs.tick(3)
+
+    @pl.loop(0, n // CHUNK)
+    def _(r):
+        at = pl.ds(pl.multiple_of(r * CHUNK, CHUNK), CHUNK)
+        hat, inv = norm_parts(x[at, :].astype(F32))
+        d = dn[at, :]
+        vs[0, G_AG:G_AG + 1, :] += colsum(d * hat)
+        vs[0, G_AB:G_AB + 1, :] += colsum(d)
+        d_in[at, :] = (d_after[at, :] + norm_back(hat, inv, d * vec[V_AG:V_AG + 1, :])).astype(BF)
+
+    steps = [(p.dp, p.other), (p.xn, p.mp), (p.yn, p.mp), (p.z1, p.mp), (p.z2, p.mp)]
+
+    def hop(i):
+        return remote(vs.at[i], vr.at[i], vss.at[i], vsr.at[i], *steps[i])
+
+    hop(0).start()
+    for i in range(5):
+        rs.tick(4 + i)
+        hop(i).wait()
+        v = vs[i] + vr[i]
+        if i < 4:
+            vs[i + 1] = v
+            hop(i + 1).start()
+        else:
+            vout[...] = v
+    for t in range(9, 4 * C + 2):
+        rs.tick(t)
+    for t in range(4 * C):
+        rs.finish(t)
+
+
+def tail(vec, x, activ, mixed, d_proj, d_branch, d_after, wqkv, vsum, C=2):
+    n, width = x.shape
+    rows = width // 32
+    sds = jax.ShapeDtypeStruct
+    full = pltpu.VMEM((4, 2, rows, 2 * width), BF)
+    part = pltpu.VMEM((4, 1, rows, 2 * width), BF)
+    return pl.pallas_call(
+        functools.partial(tail_kernel, C),
+        out_shape=(
+            sds((rows, 3 * width), F32),
+            sds((rows, width), F32),
+            sds((n, width), BF),
+            sds((24, width), F32),
+        ),
+        in_specs=[VM] * 9,
+        out_specs=(VM,) * 4,
+        scratch_shapes=[
+            pltpu.VMEM((width, width), F32),
+            pltpu.VMEM((2, 4, 16, rows, width), BF),
+            pltpu.VMEM((4, 16, rows, width), BF),
+            pltpu.VMEM((2, 16, rows, 2 * width), BF),
+            full, full, part, part, full, full,
+            pltpu.VMEM((n, width), F32),
+            pltpu.VMEM((5, 24, width), F32),
+            pltpu.VMEM((5, 24, width), F32),
+            DMA((6, C, 4)), DMA((6, C, 4)), DMA((4,)), DMA((4,)), DMA((5,)), DMA((5,)),
+        ],
+        compiler_params=pltpu.CompilerParams(
+            collective_id=2, has_side_effects=True, vmem_limit_bytes=60 << 20
+        ),
+        name="tail",
+    )(vec, x, activ, mixed, d_proj, d_branch, d_after, wqkv, vsum)
+
+
+def local_shards(
+    layer_input_rows,
+    resolution,
+    attn_gain,
+    attn_bias,
+    qkv_weight,
+    qv_bias,
+    out_weight,
+    out_bias,
+    attn_scale,
+    ffn_scale,
+    ffn_gain,
+    ffn_bias,
+    up_weight,
+    up_bias,
+    down_weight,
+    down_bias,
+    output_gradient,
+):
+    x, og = layer_input_rows, output_gradient
+    width = x.shape[1]
+    small = (
+        attn_gain, attn_bias, qv_bias, out_bias, attn_scale, ffn_scale, ffn_gain, ffn_bias, down_bias
+    )
+    proj, activ, mixed, vec, ub, fsum, bsum, grads = front(
+        resolution, small, up_bias, x, og, qkv_weight, out_weight, up_weight, down_weight
+    )
+    up_weight_grad, down_weight_grad, block_output, d_proj, d_branch, d_after, vsum = back(
+        resolution, vec, ub, x, og, fsum, bsum, proj, mixed, out_weight, grads
+    )
+    qkv_out, out_out, input_grad, v = tail(
+        vec, x, activ, mixed, d_proj, d_branch, d_after, qkv_weight, vsum
+    )
+    return (
+        block_output,
+        input_grad,
+        v[G_AG],
+        v[G_AB],
+        qkv_out,
+        v[G_QB:G_QB + 2],
+        out_out,
+        v[G_OB],
+        v[G_AS],
+        v[G_FS],
+        v[G_FG:G_FG + 2],
+        v[G_FB:G_FB + 2],
+        up_weight_grad,
+        v[G_UB:G_UB + 8].reshape(2, 4 * width),
+        down_weight_grad,
+        v[G_DB:G_DB + 2],
+    )
+
+
 def solution(mesh):
     placed = (
         P(("dp", "mp"), None),
@@ -342,8 +1306,9 @@
         P(),
         P(("dp", "mp"), None),
     )
+    fast = mesh.shape["dp"] == 16 and mesh.shape["mp"] == 2
     return jax.shard_map(
-        shards,
+        local_shards if fast else shards,
         mesh=mesh,
         in_specs=placed,
         out_specs=(

time: 1050 us -> 268 us (0.26)
  waiting for transfers between devices: 616 us -> 0 us
  Pallas kernels: 0 us -> 256 us
  matrix products: 153 us -> 0 us
  other arithmetic: 97.1 us -> 0 us
  blocking collectives: 86.8 us -> 0 us
  local copies, waits for them, and re-layouts: 56.4 us -> 10.7 us
  starting transfers between devices: 19.2 us -> 0 us
  between operations: 16.3 us -> 1.37 us
    reduce_scatter x6 -> x0, waiting for transfers between devices: 430 us -> none  [the longest x1 177 us: shards(): lax.psum_scatter(expert_pick * own_down_grad[None], 'dp', scatter_dimensi...]
    pallas_call x0 -> x3, Pallas kernels: none -> 256 us  [the longest x1 110 us: front(): pl.pallas_call(functools.partial(front_kernel, C), out_shape=(sds((n, 3 *...]
    dot_general x21 -> x0, matrix products: 153 us -> none  [the longest x1 28.1 us: shards(): jnp.dot(paired, own_up, preferred_element_type=jnp.float32) + own_up_bias]
    all_gather x4 -> x0, waiting for transfers between devices: 95.9 us -> none  [the longest x1 53 us: shards(): lax.all_gather(down_weight, 'dp', axis=1, tiled=True)]
    all_to_all x3 -> x0, waiting for transfers between devices: 87.7 us -> none  [the longest x1 40.2 us: shards(): lax.all_to_all(to_slots(d_expert), 'dp', split_axis=0, concat_axis=0, til...]
    psum x1 -> x0, blocking collectives: 44.6 us -> none  [shards(): lax.psum((attn_gain_grad, attn_bias_grad, qv_bias_grad, out_bias_grad, at...]
    all_to_all x1 -> x0, blocking collectives: 42.2 us -> none  [shards(): lax.all_to_all(to_slots(sent_rows), 'dp', split_axis=0, concat_axis=0, ti...]
    convert_element_type x8 -> x0, other arithmetic: 26.1 us -> none  [the longest x1 14.3 us: attend_back(): d_scores = (probs_full * (d_probs - row_delta)).astype(jnp.bfloat16)]
  transfers between devices with their start and end apart: 13 -> 0, of which waited for: 9 -> 0; matrix products, arithmetic and copies ran while one was open for 19% -> 0% of each run, Pallas kernels for 0% -> 0%
where the time goes in v1:
time: 268 us
  Pallas kernels  256 us (96%)
  local copies, waits for them, and re-layouts  10.7 us (4%)
    pallas_call x1, Pallas kernels, front(): pl.pallas_call(functools.partial(front_kernel, C), out_shape=(sds((n, 3 *...  110 us
    pallas_call x1, Pallas kernels, back(): pl.pallas_call(functools.partial(back_kernel, C), out_shape=(sds((2, rows...  91.8 us
    pallas_call x1, Pallas kernels, tail(): pl.pallas_call(functools.partial(tail_kernel, C), out_shape=(sds((rows, 3...  53.8 us
    unnamed x16, local copies, waits for them, and re-layouts  6.12 us

profile of v1, /device:TPU:0, one launch (start us, length us, event | category | flops | bytes accessed | tf_op | source)
XLA Modules:
  0.0 267.7 jit_solution(12334045232586416918)
XLA Ops:
  1.3 110.1 %front.1 = (bf16[640,2304]{1,0:T(8,128)(2,1)}, bf16[640,768]{1,0:T(8,128)(2,1)}, bf16[640,768]{1,0:T(8,128)(2,1)}, f32[16,768]{1,0:T(8,128)}, f32[8,768]{1,0:T(8...) custom-call(s32[1]{0:T(128)S(6)} %copy.39.res_ref, f32[768]{0:T(1024)} %a_gain.1, ...), custom_call_target="tpu_custom_call" | custom-call | tf_op jit(solution)/shard_map/front/pallas_call | solution.py:898
  111.4 91.8 %back.1 = (f32[2,48,1536]{2,1,0:T(8,128)}, f32[2,48,1536]{2,1,0:T(8,128)}, bf16[640,768]{1,0:T(8,128)(2,1)}, bf16[640,2304]{1,0:T(8,128)(2,1)}, bf16[640,768]{1,...) custom-call(s32[1]{0:T(128)S(6)} %copy.39.res_ref, f32[16,768]{1,0:T(8,128)} %get-tuple-element.35.vec, ...), custom_call_target="tpu_custom_call" | custom-call | tf_op jit(solution)/shard_map/back/pallas_call | solution.py:1076
  203.2 0.0 copy-start
  203.2 53.8 %tail.1 = (f32[24,2304]{1,0:T(8,128)}, f32[24,768]{1,0:T(8,128)}, bf16[640,768]{1,0:T(8,128)(2,1)}, f32[24,768]{1,0:T(8,128)}) custom-call(f32[16,768]{1,0:T(8,128)} %get-tuple-element.35.vec, bf16[640,768]{1,0:T(8,128)(2,1)} %x.5, bf16[640,768]{1,0:T(8,128)(2,1)} %get-tuple-element.43.activ, bf16[640,768]{1,0:T(8,128)(2,1)} %get-tuple-element.40.mixed_h.mixed, ...), custom_call_target="tpu_custom_call" | custom-call | tf_op jit(solution)/shard_map/tail/pallas_call | solution.py:1208
  257.0 0.0 copy-start.3
  257.0 0.0 copy-start.4
  257.0 0.0 copy-start.2
  257.0 0.0 copy-start.1
  257.0 1.7 slice_reduce_fusion
  258.7 0.7 slice.38
  259.4 1.5 fusion
  260.9 0.6 reshape.35
  261.6 0.0 copy-done
  261.6 0.9 copy.40
  262.5 2.2 copy.41
  264.7 0.0 copy-done.3
  264.7 0.7 copy.42
  265.4 0.0 copy-done.4
  265.4 0.6 copy.43
  266.0 0.0 copy-done.2
  266.0 0.8 copy.44
  266.9 0.0 copy-done.1
  266.9 0.8 copy.45
Async XLA Ops:
  203.2 58.4 %copy-start = (bf16[640,768]{1,0:T(8,128)(2,1)S(1)}, bf16[640,768]{1,0:T(8,128)(2,1)}, u32[]{:S(2)}) copy-start(bf16[640,768]{1,0:T(8,128)(2,1)} %get-tuple-element.79) | copy-start | bytes 2949124
  257.0 7.7 %copy-start.3 = (f32[24,2304]{1,0:T(8,128)S(1)}, f32[24,2304]{1,0:T(8,128)}, u32[]{:S(2)}) copy-start(f32[24,2304]{1,0:T(8,128)} %get-tuple-element.83) | copy-start | bytes 663556
  257.0 8.4 %copy-start.4 = (f32[24,768]{1,0:T(8,128)S(1)}, f32[24,768]{1,0:T(8,128)}, u32[]{:S(2)}) copy-start(f32[24,768]{1,0:T(8,128)} %get-tuple-element.85) | copy-start | bytes 221188
  257.0 9.0 %copy-start.2 = (f32[2,48,1536]{2,1,0:T(8,128)S(1)}, f32[2,48,1536]{2,1,0:T(8,128)}, u32[]{:S(2)}) copy-start(f32[2,48,1536]{2,1,0:T(8,128)} %get-tuple-element.91) | copy-start | bytes 1769476
  257.0 9.9 %copy-start.1 = (f32[2,48,1536]{2,1,0:T(8,128)S(1)}, f32[2,48,1536]{2,1,0:T(8,128)}, u32[]{:S(2)}) copy-start(f32[2,48,1536]{2,1,0:T(8,128)} %get-tuple-element.93) | copy-start | bytes 1769476

commit v2 on v1

--- a/solution.py
+++ b/solution.py
@@ -422,6 +422,11 @@
         s.z1 = s.dp + 4 - 8 * (s.z % 2)
         s.z2 = s.dp + 8 - 16 * (s.z // 2)
         s.other = 1 - s.mp
+        s.q = s.y * 2 + s.x
+        s.dn = s.dp + 3 - 2 * s.x - 4 * s.y
+        s.plane = [
+            (s.xn, s.y * 2 + 1 - s.x), (s.yn, 2 - 2 * s.y + s.x), (s.dn, 3 - 2 * s.y - s.x)
+        ]
 
     def barrier(s, far=False):
         bar = pltpu.get_barrier_semaphore()
@@ -433,8 +438,7 @@
         sig(s.xn, s.mp)
         sig(s.yn, s.mp)
         sig(dp, s.other)
-        if far:
-            sig(s.z2, s.mp)
+        sig(s.z2 if far else s.dn, s.mp)
 
         @pl.when(z > 0)
         def _():
@@ -444,7 +448,7 @@
         def _():
             sig(dp + 4, s.mp)
 
-        pl.semaphore_wait(bar, 4 + int(far) + ((z + 1) // 2) % 2)
+        pl.semaphore_wait(bar, 5 + ((z + 1) // 2) % 2)
 
 
 def remote(src, dst, ss, sr, dev, core):
@@ -462,7 +466,7 @@
         s.col = place.y * 2 + place.x
 
     def cp(s, kind, c, u, owner, dev, half=None):
-        h = slice(0, 4) if half is None else slice(2 * half, 2 * half + 2)
+        h = slice(0, 2) if half is None else slice(half, half + 1)
         at = pl.ds(pl.multiple_of(owner * s.rows, 16), s.rows)
         w = s.g.at[h, at, pl.ds(pl.multiple_of(c * s.ck, 128), s.ck)]
         rk = 0 if kind == 1 else kind
@@ -533,6 +537,138 @@
         @pl.when((u >= z) & (z > 0))
         def _():
             s.cp(1, c, u, own, dp).wait_send()
+
+
+class CaptionGather:
+    def __init__(s, place, own, wc, lsem, ps, pr, zs, zr):
+        s.p, s.own, s.wc, s.lsem, s.ps, s.pr, s.zs, s.zr = place, own, wc, lsem, ps, pr, zs, zr
+        s.rows, s.quarter = own.shape[1], wc.shape[2]
+        s.at = pl.ds(pl.multiple_of(place.dp * s.rows, 16), s.rows)
+
+    def part(s, q):
+        return s.own.at[:, :, pl.ds(pl.multiple_of(q * s.quarter, 128), s.quarter)]
+
+    def keep(s):
+        return pltpu.make_async_copy(s.part(s.p.q), s.wc.at[:, s.at, :], s.lsem)
+
+    def flat(s, i):
+        dev, q = s.p.plane[i]
+        return remote(s.part(q), s.wc.at[:, s.at, :], s.ps.at[i], s.pr.at[i], dev, s.p.mp)
+
+    def start(s):
+        s.keep().start()
+        for i in range(3):
+            s.flat(i).start()
+
+    def hop(s, kind, u, dev):
+        n = 4 * s.rows
+        w = s.wc.at[:, pl.ds(pl.multiple_of(u * n, 16), n), :]
+        return remote(w, w, s.zs.at[kind, u], s.zr.at[u], dev, s.p.mp)
+
+    def step(s, k):
+        z, dp = s.p.z, s.p.dp
+        u = dyn_unit(z, k)
+        if isinstance(k, int) and k == 0:
+            s.keep().wait()
+            for i in range(3):
+                s.flat(i).wait()
+        else:
+            s.hop(0, u, dp).wait_recv()
+
+        @pl.when((u <= z) & (z < 3))
+        def _():
+            s.hop(0, u, dp + 4).start()
+
+        @pl.when((u >= z) & (z > 0))
+        def _():
+            s.hop(1, u, dp - 4).start()
+
+    def finish(s):
+        z, dp = s.p.z, s.p.dp
+        for k in range(4):
+            u = dyn_unit(z, k)
+
+            @pl.when((u <= z) & (z < 3))
+            def _():
+                s.hop(0, u, dp + 4).wait_send()
+
+            @pl.when((u >= z) & (z > 0))
+            def _():
+                s.hop(1, u, dp - 4).wait_send()
+
+
+class CaptionScatter:
+    def __init__(s, place, g, bu, bd, got, ps, pr, zs, zr, out):
+        s.p, s.g, s.bu, s.bd, s.got, s.out = place, g, bu, bd, got, out
+        s.ps, s.pr, s.zs, s.zr = ps, pr, zs, zr
+        s.rows = g.shape[1] // 16
+
+    def win(s, u):
+        n = 4 * s.rows
+        return s.g.at[:, pl.ds(pl.multiple_of(u * n, 16), n), :]
+
+    def up(s, u):
+        return remote(s.win(u), s.bu.at[u], s.zs.at[0, u], s.zr.at[0, u], s.p.dp + 4, s.p.mp)
+
+    def down(s, u):
+        return remote(s.win(u), s.bd.at[u], s.zs.at[1, u], s.zr.at[1, u], s.p.dp - 4, s.p.mp)
+
+    def owner(s, q):
+        at = pl.multiple_of((s.p.z * 4 + q) * s.rows, 16)
+        return s.g.at[:, pl.ds(at, s.rows), :]
+
+    def flat(s, i):
+        dev, q = s.p.plane[i]
+        return remote(s.owner(q), s.got.at[i], s.ps.at[i], s.pr.at[i], dev, s.p.mp)
+
+    def step(s, k):
+        z = s.p.z
+        u = dyn_unit(z, k)
+        o = s.win(u)
+
+        def go(pred, wu, wd, send):
+            @pl.when(pred)
+            def _():
+                v = o[...].astype(F32)
+                if wu:
+                    s.up(u).wait_recv()
+                    v = v + s.bu.at[u][...].astype(F32)
+                if wd:
+                    s.down(u).wait_recv()
+                    v = v + s.bd.at[u][...].astype(F32)
+                if wu or wd:
+                    o[...] = v.astype(BF)
+                if send is not None:
+                    send(u).start()
+
+        if k > 0:
+            go((u > z) & (z > 0), True, False, s.up)
+            go((u > z) & (z == 0), False, False, s.up)
+            go((u < z) & (z < 3), False, True, s.down)
+            go((u < z) & (z == 3), False, False, s.down)
+        else:
+            go(z == 0, False, True, None)
+            go(z == 3, True, False, None)
+            go((z > 0) & (z < 3), True, True, None)
+            for i in range(3):
+                s.flat(i).start()
+
+    def finish(s):
+        own = s.owner(s.p.q)
+        s.out(s.p.q, own[0].astype(F32), own[1].astype(F32))
+        for i in range(3):
+            s.flat(i).wait()
+            s.out(s.p.plane[i][1], s.got[i, 0].astype(F32), s.got[i, 1].astype(F32))
+        for k in range(1, 4):
+            u = dyn_unit(s.p.z, k)
+
+            @pl.when(u > s.p.z)
+            def _():
+                s.up(u).wait_send()
+
+            @pl.when(u < s.p.z)
+            def _():
+                s.down(u).wait_send()
 
 
 class RS:
@@ -677,19 +813,28 @@
 def front_kernel(
     C, res_ref, a_gain, a_bias, qv_bias, o_bias, a_scale, f_scale, f_gain, f_bias, dn_bias, up_bias,
     x, og, wqkv, wout, up_ref, down_ref,
-    proj, activ, mixed, vec, ub, fsum, bsum, grads,
-    g, bias, qkvb, xall, gall, xt, gt, xct, gct, accf, accb, rcv, stage, hid, dpre, ubg,
-    lsem, ss, sr, ps, pr,
+    proj, activ, mixed, vec, ub, fsum, bsum, cgrads, grads,
+    g, wc, cown, bias, qkvb, xall, gall, xt, gt, cr, crt, accf, accb, rcv, stage, hid, dpre, ubg,
+    chid, cdpre, pc, prc, prq,
+    lsem, ss, sr, ps, pr, cs, cg_r, zs, zr, bs, br,
 ):
     p = Place()
     n, width = x.shape
     res = res_ref[0]
     ag = AG(p, g, ss, sr, C)
     mine = pl.ds(pl.multiple_of(p.dp * ag.rows, 16), ag.rows)
-    loads = load_all([(up_ref, g.at[0:2, mine, :]), (down_ref, g.at[2:4, mine, :])], lsem)
+    loads = load_all(
+        [
+            (up_ref.at[1], g.at[0, mine, :]), (down_ref.at[1], g.at[1, mine, :]),
+            (up_ref.at[0], cown.at[0]), (down_ref.at[0], cown.at[1]),
+        ],
+        lsem,
+    )
     p.barrier()
     for c in loads:
         c.wait()
+    capg = CaptionGather(p, cown, wc, lsem.at[4], cs.at[0], cg_r.at[0], zs, zr)
+    capg.start()
     for c in range(C):
         ag.send(0, c, True)
 
@@ -719,6 +864,7 @@
         proj[:, at] = (v + qkvb[:, at]).astype(BF)
 
     fill_bias(res, bias)
+    capg.step(0)
     masks = [half_mask(0, 0.125), half_mask(1, 0.125)]
     first = iota((1, 128), 1) < 64
 
@@ -730,6 +876,10 @@
         @pl.when(h > 0)
         def _():
             ag.tick(h - 1)
+
+        @pl.when((h > 0) & (h % 2 == 0))
+        def _():
+            capg.step(h // 2)
 
         q, k, v = proj[:, cols(0)], proj[:, cols(width)], proj[:, cols(2 * width)]
         outs = []
@@ -741,6 +891,7 @@
         mixed[:, cols(0)] = jnp.where(first, outs[0], outs[1]).astype(BF)
 
     ag.tick(5)
+    capg.step(3)
     half = 256
 
     @pl.loop(0, width // half)
@@ -749,7 +900,7 @@
         accf[:n, at] = jnp.dot(mixed[...], wout[:, at], preferred_element_type=F32)
 
     img = p.mp * n
-    caps = 2 * n + p.mp * CAPS
+    caps = p.mp * 4 * CAPS + p.q * CAPS
 
     @pl.loop(0, n // CHUNK)
     def _(r):
@@ -769,8 +920,21 @@
     pick = (iota((CAPS, n), 1) == caption_place(res, iota((CAPS, 1), 0))).astype(F32).astype(BF)
     at_img = pl.ds(pl.multiple_of(img, 128), n)
     at_cap = pl.ds(pl.multiple_of(caps, 16), CAPS)
-    for ref in (xall, gall):
-        ref[at_cap, :] = jnp.dot(pick, ref[at_img, :], preferred_element_type=F32).astype(BF)
+    for i, ref in enumerate((xall, gall)):
+        cr[i, at_cap, :] = jnp.dot(pick, ref[at_img, :], preferred_element_type=F32).astype(BF)
+
+    def rows_to(i):
+        w = cr.at[:, at_cap, :]
+        return remote(w, w, cs.at[1, i], cg_r.at[1, i], p.plane[i][0], p.mp)
+
+    def relay(i):
+        q = p.q if i == 3 else p.plane[i][1]
+        w = cr.at[:, pl.ds(pl.multiple_of(p.mp * 4 * CAPS + q * CAPS, 16), CAPS), :]
+        return remote(w, w, bs.at[i], br.at[i], p.dp, p.other)
+
+    for i in range(3):
+        rows_to(i).start()
+    relay(3).start()
 
     @pl.loop(0, n // CHUNK)
     def _(r):
@@ -780,8 +944,8 @@
         gall[to, :] = (gall[to, :].astype(F32) * vis).astype(BF)
 
     pairs = []
-    for i, (ref, at) in enumerate(((xall, at_img), (xall, at_cap), (gall, at_img), (gall, at_cap))):
-        w = ref.at[at, :]
+    for i, ref in enumerate((xall, gall)):
+        w = ref.at[at_img, :]
         pairs.append(remote(w, w, ps.at[i], pr.at[i], p.dp, p.other))
         pairs[-1].start()
     ag.tick(6)
@@ -796,28 +960,90 @@
             at = pl.ds(pl.multiple_of(r * CHUNK, CHUNK), CHUNK)
             dst[:, at] = src[at, :].T
 
-    xct[...] = xall[2 * n:, :].T
-    gct[...] = gall[2 * n:, :].T
+    for i in range(3):
+        rows_to(i).wait()
+        relay(i).start()
     ag.tick(7)
     ck = ag.ck
 
     def saved(c):
         return pltpu.make_async_copy(stage, grads.at[:, :, c * ck:(c + 1) * ck], lsem.at[2])
 
-    def rows_step(c, expert, at):
-        here = slice(c * ck, (c + 1) * ck)
-        up, down = g[expert, :, here], g[2 + expert, :, here]
-        v = jnp.dot(xall[at, :], up, preferred_element_type=F32) + up_bias[expert:expert + 1, here]
-        dh = jnp.dot(gall[at, :], down, preferred_element_type=F32)
+    def gelu_pair(v, dh):
         cdf = 0.5 * (1.0 + lax.erf(v * (0.5 ** 0.5)))
         slope = cdf + v * (jnp.exp(v * v * -0.5) * 0.3989422804014327)
-        h_low = (v * cdf).astype(BF)
-        d_low = (dh * slope).astype(BF)
+        return (v * cdf).astype(BF), (dh * slope).astype(BF)
+
+    def rows_step(c, at):
+        here = slice(c * ck, (c + 1) * ck)
+        up, down = g[0, :, here], g[1, :, here]
+        v = jnp.dot(xall[at, :], up, preferred_element_type=F32) + up_bias[1:2, here]
+        dh = jnp.dot(gall[at, :], down, preferred_element_type=F32)
+        h_low, d_low = gelu_pair(v, dh)
         hid[at, :] = h_low
         dpre[at, :] = d_low
         accf[at, :] += lax.dot_general(h_low, down, NT, preferred_element_type=F32)
         accb[at, :] += lax.dot_general(d_low, up, NT, preferred_element_type=F32)
-        ubg[expert:expert + 1, here] += colsum(d_low.astype(F32))
+        ubg[1:2, here] += colsum(d_low.astype(F32))
+
+    quarter = wc.shape[2]
+    my_cols = pl.ds(pl.multiple_of(p.q * quarter, 128), quarter)
+    cap_all = 4 * CAPS
+
+    def caption_pair():
+        w = pc.at[:, pl.ds(pl.multiple_of(p.other * cap_all, 16), cap_all), :]
+        return remote(w, prc, ps.at[4], pr.at[4], p.dp, p.other)
+
+    def caption_flat(i):
+        dev, q = p.plane[i]
+        w = pc.at[:, pl.ds(pl.multiple_of(p.mp * cap_all + q * CAPS, 16), CAPS), :]
+        return remote(w, prq.at[i], cs.at[2, i], cg_r.at[2, i], dev, p.mp)
+
+    def captions():
+        for i in range(4):
+            relay(i).wait()
+
+        @pl.loop(0, 5)
+        def _(r):
+            at = pl.ds(pl.multiple_of(r * CHUNK, CHUNK), CHUNK)
+            for i in range(2):
+                crt[i, :, at] = cr[i, at, :].T
+
+        @pl.loop(0, 2)
+        def _(r):
+            at = pl.ds(pl.multiple_of(r * cap_all, 16), cap_all)
+            v = jnp.dot(cr[0, at, :], wc[0], preferred_element_type=F32) + up_bias[0:1, my_cols]
+            dh = jnp.dot(cr[1, at, :], wc[1], preferred_element_type=F32)
+            h_low, d_low = gelu_pair(v, dh)
+            chid[at, :] = h_low
+            cdpre[at, :] = d_low
+            pc[0, at, :] = lax.dot_general(h_low, wc[1], NT, preferred_element_type=F32).astype(BF)
+            pc[1, at, :] = lax.dot_general(d_low, wc[0], NT, preferred_element_type=F32).astype(BF)
+            ubg[0:1, my_cols] += colsum(d_low.astype(F32))
+
+        caption_pair().start()
+
+        @pl.loop(0, width // 256)
+        def _(r):
+            at = pl.ds(pl.multiple_of(r * 256, 256), 256)
+            cgrads[0, at, :] = jnp.dot(
+                crt[0, at, :], cdpre[...], preferred_element_type=F32
+            ).astype(BF)
+            cgrads[1, at, :] = jnp.dot(
+                crt[1, at, :], chid[...], preferred_element_type=F32
+            ).astype(BF)
+
+        caption_pair().wait()
+
+        @pl.loop(0, 4)
+        def _(r):
+            at = pl.ds(pl.multiple_of(p.mp * cap_all + r * CAPS, 16), CAPS)
+            got = pl.ds(pl.multiple_of(r * CAPS, 16), CAPS)
+            for i in range(2):
+                pc[i, at, :] = (pc[i, at, :].astype(F32) + prc[i, got, :].astype(F32)).astype(BF)
+
+        for i in range(3):
+            caption_flat(i).start()
 
     back_pairs = []
     for c in range(C):
@@ -825,68 +1051,61 @@
 
         @pl.loop(0, 2 * n // 256)
         def _(r):
-            rows_step(c, 1, pl.ds(pl.multiple_of(r * 256, 256), 256))
-
-        rows_step(c, 0, slice(2 * n, 2 * n + 2 * CAPS))
+            rows_step(c, pl.ds(pl.multiple_of(r * 256, 256), 256))
+
         if c == 0:
             ag.tick(8)
         if c == C - 1:
             theirs_img = pl.ds(pl.multiple_of(p.other * n, 128), n)
-            theirs_cap = pl.ds(pl.multiple_of(2 * n + p.other * CAPS, 16), CAPS)
             for i, (acc, low) in enumerate(((accf, xall), (accb, gall))):
-                @pl.loop(0, 9)
+                @pl.loop(0, 2 * n // CHUNK)
                 def _(r):
-                    at = pl.ds(pl.multiple_of(r * 160, 16), 160)
+                    at = pl.ds(pl.multiple_of(r * CHUNK, CHUNK), CHUNK)
                     low[at, :] = acc[at, :].astype(BF)
 
-                for j, (at, lo, size) in enumerate(((theirs_img, 0, n), (theirs_cap, n, CAPS))):
-                    k = 2 * i + j
-                    to = rcv.at[pl.ds(i * (n + CAPS) + lo, size), :]
-                    back_pairs.append(
-                        remote(low.at[at, :], to, ps.at[4 + k], pr.at[4 + k], p.dp, p.other)
-                    )
-                    back_pairs[-1].start()
+                to = rcv.at[i]
+                back_pairs.append(
+                    remote(low.at[theirs_img, :], to, ps.at[2 + i], pr.at[2 + i], p.dp, p.other)
+                )
+                back_pairs[-1].start()
         if c > 0:
             saved(c - 1).wait()
 
         @pl.loop(0, width // 256)
         def _(r):
             at = pl.ds(pl.multiple_of(r * 256, 256), 256)
-            im = slice(0, 2 * n)
-            cp = slice(2 * n, 2 * n + 2 * CAPS)
-            for i, (l, rr, rows) in enumerate(
-                ((xct, dpre, cp), (xt, dpre, im), (gct, hid, cp), (gt, hid, im))
-            ):
-                stage[i, at, :] = jnp.dot(
-                    l[at, :], rr[rows, :], preferred_element_type=F32
-                ).astype(BF)
+            stage[0, at, :] = jnp.dot(xt[at, :], dpre[...], preferred_element_type=F32).astype(BF)
+            stage[1, at, :] = jnp.dot(gt[at, :], hid[...], preferred_element_type=F32).astype(BF)
 
         saved(c).start()
         if c == 0:
             ag.forward(3, C - 1)
+            captions()
     ub[...] = jnp.zeros(ub.shape, F32)
     for e in range(2):
         for j in range(2):
             ub[pl.ds(e * 4 + p.mp * 2 + j, 1), :] = ubg[e:e + 1, j * width:(j + 1) * width]
     for c in back_pairs:
         c.wait()
+    for i in range(3):
+        caption_flat(i).wait()
     for i, (low, out) in enumerate(((xall, fsum), (gall, bsum))):
-        off = i * (n + CAPS)
-
         @pl.loop(0, n // CHUNK)
         def _(r):
             base = r * CHUNK
             at = pl.ds(pl.multiple_of(base, CHUNK), CHUNK)
             own = low[pl.ds(pl.multiple_of(img + base, CHUNK), CHUNK), :].astype(F32)
-            got = rcv[pl.ds(pl.multiple_of(off + base, 16), CHUNK), :].astype(F32)
-            out[at, :] = (own + got).astype(BF)
-
-        own = low[at_cap, :].astype(F32)
-        out[n:, :] = (own + rcv[off + n:off + n + CAPS, :].astype(F32)).astype(BF)
+            out[at, :] = (own + rcv[i, at, :].astype(F32)).astype(BF)
+
+        own = pc[i, at_cap, :].astype(F32)
+        for j in range(3):
+            own = own + prq[j, i].astype(F32)
+        out[n:, :] = own.astype(BF)
     saved(C - 1).wait()
     for k in range(4):
         for c in range(C):
             ag.finish(k, c)
+    capg.finish()
 
 
 def front(res, small, up_bias, x, og, wqkv, wout, up, down, C=3):
@@ -894,7 +1113,9 @@
     _, rows, hid = up.shape
     ck = hid // C
     sds = jax.ShapeDtypeStruct
-    wide = 2 * (n + CAPS)
+    wide = 2 * n
+    quarter = hid // 4
+    caps = 8 * CAPS
     return pl.pallas_call(
         functools.partial(front_kernel, C),
         out_shape=(
@@ -905,28 +1126,37 @@
             sds((8, width), F32),
             sds((n + CAPS, width), BF),
             sds((n + CAPS, width), BF),
-            sds((4, rows * 16, hid), BF),
+            sds((2, rows * 16, quarter), BF),
+            sds((2, rows * 16, hid), BF),
         ),
         in_specs=[SM] + [VM] * 14 + [ANY, ANY],
-        out_specs=(VM,) * 7 + (ANY,),
+        out_specs=(VM,) * 8 + (ANY,),
         scratch_shapes=[
-            pltpu.VMEM((4, rows * 16, hid), BF),
+            pltpu.VMEM((2, rows * 16, hid), BF),
+            pltpu.VMEM((2, rows * 16, quarter), BF),
+            pltpu.VMEM((2, rows, hid), BF),
             pltpu.VMEM((n, n), F32),
             pltpu.VMEM((1, 3 * width), F32),
             pltpu.VMEM((wide, width), BF),
             pltpu.VMEM((wide, width), BF),
-            pltpu.VMEM((width, 2 * n), BF),
-            pltpu.VMEM((width, 2 * n), BF),
-            pltpu.VMEM((width, 2 * CAPS), BF),
-            pltpu.VMEM((width, 2 * CAPS), BF),
+            pltpu.VMEM((width, wide), BF),
+            pltpu.VMEM((width, wide), BF),
+            pltpu.VMEM((2, caps, width), BF),
+            pltpu.VMEM((2, width, caps), BF),
             pltpu.VMEM((wide, width), F32),
             pltpu.VMEM((wide, width), F32),
-            pltpu.VMEM((wide, width), BF),
-            pltpu.VMEM((4, rows * 16, ck), BF),
+            pltpu.VMEM((2, n, width), BF),
+            pltpu.VMEM((2, rows * 16, ck), BF),
             pltpu.VMEM((wide, ck), BF),
             pltpu.VMEM((wide, ck), BF),
             pltpu.VMEM((2, hid), F32),
-            DMA((3,)), DMA((6, C, 4)), DMA((6, C, 4)), DMA((8,)), DMA((8,)),
+            pltpu.VMEM((caps, quarter), BF),
+            pltpu.VMEM((caps, quarter), BF),
+            pltpu.VMEM((2, caps, width), BF),
+            pltpu.VMEM((2, caps // 2, width), BF),
+            pltpu.VMEM((3, 2, CAPS, width), BF),
+            DMA((5,)), DMA((6, C, 4)), DMA((6, C, 4)), DMA((5,)), DMA((5,)),
+            DMA((3, 3)), DMA((3, 3)), DMA((2, 4)), DMA((4,)), DMA((4,)), DMA((4,)),
         ],
         compiler_params=pltpu.CompilerParams(
             collective_id=0, has_side_effects=True, vmem_limit_bytes=67043328
@@ -936,25 +1166,34 @@
 
 
 def back_kernel(
-    C, res_ref, vec, ub, x, og, fsum, bsum, proj_h, mixed_h, wout, grads_h,
+    C, res_ref, vec, ub, x, og, fsum, bsum, proj_h, mixed_h, wout, cgrads_h, grads_h,
     out_up, out_down, block, d_proj, d_branch, d_after, vsum,
-    g, bx, by, bdx, bdy, bzu, bzd, proj, mixed, capf, branch, d_mixed, bias,
-    lsem, ss, sr,
+    g, bx, by, bdx, bdy, bzu, bzd, cg, cbu, cbd, cgot, proj, mixed, capf, branch, d_mixed, bias,
+    lsem, ss, sr, cps, cpr, czs, czr,
 ):
     p = Place()
     n, width = x.shape
     res = res_ref[0]
-    loads = load_all([(grads_h, g), (proj_h, proj), (mixed_h, mixed)], lsem)
+    loads = load_all([(grads_h, g), (proj_h, proj), (mixed_h, mixed), (cgrads_h, cg)], lsem)
     p.barrier()
 
     def write(c, v):
         at = pl.ds(pl.multiple_of(c * (g.shape[2] // C), 128), g.shape[2] // C)
-        out_up[:, :, at] = v[:2]
-        out_down[:, :, at] = v[2:]
+        out_up[1, :, at] = v[0]
+        out_down[1, :, at] = v[1]
+
+    def caption_out(q, up, down):
+        quarter = cg.shape[2]
+        at = pl.ds(pl.multiple_of(q * quarter, 128), quarter)
+        out_up[0, :, at] = up
+        out_down[0, :, at] = down
 
     rs = RS(p, g, (bx, by, bdx, bdy, bzu, bzd), ss, sr, C, write)
+    cap = CaptionScatter(p, cg, cbu, cbd, cgot, cps, cpr, czs, czr, caption_out)
     loads[0].wait()
     rs.tick(0)
+    loads[3].wait()
+    cap.step(3)
     loads[1].wait()
     loads[2].wait()
     fill_bias(res, bias)
@@ -1017,6 +1256,7 @@
         add(G_OB, db.astype(F32))
 
     rs.tick(1)
+    cap.step(2)
 
     @pl.loop(0, width // half)
     def _(j):
@@ -1034,6 +1274,14 @@
         rs.s1(t)
         rs.s2(t - 1)
         rs.s3(t - 2)
+
+        @pl.when(h == 0)
+        def _():
+            cap.step(1)
+
+        @pl.when(h == 3)
+        def _():
+            cap.step(0)
 
         def cols(base):
             return pl.ds(pl.multiple_of(base + h * 128, 128), 128)
@@ -1063,11 +1311,13 @@
 
     rs.tick(4 * C)
     rs.tick(4 * C + 1)
+    cap.finish()
     for t in range(4 * C):
         rs.finish(t)
 
 
-def back(res, vec, ub, x, og, fsum, bsum, proj, mixed, wout, grads, C=2):
+def back(res, vec, ub, x, og, fsum, bsum, proj, mixed, wout, cgrads, grads, C=2):
+    quarter = cgrads.shape[2]
     n, width = x.shape
     M, rows, hid = grads.shape[0], grads.shape[1] // 16, grads.shape[2]
     sds = jax.ShapeDtypeStruct
@@ -1084,24 +1334,28 @@
             sds((n, width), F32),
             sds((24, width), F32),
         ),
-        in_specs=[SM] + [VM] * 6 + [ANY, ANY, VM, ANY],
+        in_specs=[SM] + [VM] * 6 + [ANY, ANY, VM, ANY, ANY],
         out_specs=(VM,) * 7,
         scratch_shapes=[
             pltpu.VMEM((M, 16 * rows, hid), BF),
             full, full, part, part, full, full,
+            pltpu.VMEM((M, 16 * rows, quarter), BF),
+            pltpu.VMEM((4, M, 4 * rows, quarter), BF),
+            pltpu.VMEM((4, M, 4 * rows, quarter), BF),
+            pltpu.VMEM((3, M, rows, quarter), BF),
             pltpu.VMEM((n, 3 * width), BF),
             pltpu.VMEM((n, width), BF),
             pltpu.VMEM((2, 128, width), BF),
             pltpu.VMEM((n, width), F32),
             pltpu.VMEM((n, width), BF),
             pltpu.VMEM((n, n), F32),
-            DMA((3,)), DMA((6, C, 4)), DMA((6, C, 4)),
+            DMA((4,)), DMA((6, C, 4)), DMA((6, C, 4)), DMA((3,)), DMA((3,)), DMA((2, 4)), DMA((2, 4)),
         ],
         compiler_params=pltpu.CompilerParams(
             collective_id=1, has_side_effects=True, vmem_limit_bytes=63 << 20
         ),
         name="back",
-    )(res, vec, ub, x, og, fsum, bsum, proj, mixed, wout, grads)
+    )(res, vec, ub, x, og, fsum, bsum, proj, mixed, wout, cgrads, grads)
 
 
 def tail_kernel(
@@ -1257,11 +1511,11 @@
     small = (
         attn_gain, attn_bias, qv_bias, out_bias, attn_scale, ffn_scale, ffn_gain, ffn_bias, down_bias
     )
-    proj, activ, mixed, vec, ub, fsum, bsum, grads = front(
+    proj, activ, mixed, vec, ub, fsum, bsum, cgrads, grads = front(
         resolution, small, up_bias, x, og, qkv_weight, out_weight, up_weight, down_weight
     )
     up_weight_grad, down_weight_grad, block_output, d_proj, d_branch, d_after, vsum = back(
-        resolution, vec, ub, x, og, fsum, bsum, proj, mixed, out_weight, grads
+        resolution, vec, ub, x, og, fsum, bsum, proj, mixed, out_weight, cgrads, grads
     )
     qkv_out, out_out, input_grad, v = tail(
         vec, x, activ, mixed, d_proj, d_branch, d_after, qkv_weight, vsum

time: 268 us -> 234 us (0.87)
  Pallas kernels: 256 us -> 223 us
    pallas_call x1, Pallas kernels: 91.8 us -> 66.8 us  [back(): pl.pallas_call(functools.partial(back_kernel, C), out_shape=(sds((2, rows...]
    pallas_call x1, Pallas kernels: 110 us -> 102 us  [front(): pl.pallas_call(functools.partial(front_kernel, C), out_shape=(sds((n, 3 *...]
    unnamed x16 -> x18, local copies, waits for them, and re-layouts: 6.12 us -> 4.86 us
where the time goes in v2:
time: 234 us
  Pallas kernels  223 us (95%)
  local copies, waits for them, and re-layouts  9.41 us (4%)
    pallas_call x1, Pallas kernels, front(): pl.pallas_call(functools.partial(front_kernel, C), out_shape=(sds((n, 3 *...  102 us
    pallas_call x1, Pallas kernels, back(): pl.pallas_call(functools.partial(back_kernel, C), out_shape=(sds((2, rows...  66.8 us
    pallas_call x1, Pallas kernels, tail(): pl.pallas_call(functools.partial(tail_kernel, C), out_shape=(sds((rows, 3...  54.7 us
    unnamed x18, local copies, waits for them, and re-layouts  4.86 us

profile of v2, /device:TPU:0, one launch (start us, length us, event | category | flops | bytes accessed | tf_op | source)
XLA Modules:
  0.0 234.0 jit_solution(540722656736909701)
XLA Ops:
  1.3 101.7 %front.1 = (bf16[640,2304]{1,0:T(8,128)(2,1)}, bf16[640,768]{1,0:T(8,128)(2,1)}, bf16[640,768]{1,0:T(8,128)(2,1)}, f32[16,768]{1,0:T(8,128)}, f32[8,768]{1,0:T(8...) custom-call(s32[1]{0:T(128)S(6)} %copy.39.res_ref, ...), custom_call_target="tpu_custom_call" | custom-call | tf_op jit(solution)/shard_map/front/pallas_call | solution.py:1119
  103.0 66.8 %back.1 = (f32[2,48,1536]{2,1,0:T(8,128)}, f32[2,48,1536]{2,1,0:T(8,128)}, bf16[640,768]{1,0:T(8,128)(2,1)}, bf16[640,2304]{1,0:T(8,128)(2,1)}, bf16[640,768]{1,...) custom-call(s32[1]{0:T(128)S(6)} %copy.39.res_ref, f32[16,768]{1,0:T(8,128)} %get-tuple-element.36.vec, ...), custom_call_target="tpu_custom_call" | custom-call | tf_op jit(solution)/shard_map/back/pallas_call | solution.py:1326
  169.9 0.0 copy-start
  169.9 54.7 %tail.1 = (f32[24,2304]{1,0:T(8,128)}, f32[24,768]{1,0:T(8,128)}, bf16[640,768]{1,0:T(8,128)(2,1)}, f32[24,768]{1,0:T(8,128)}) custom-call(f32[16,768]{1,0:T(8,128)} %get-tuple-element.36.vec, bf16[640,768]{1,0:T(8,128)(2,1)} %x.5, bf16[640,768]{1,0:T(8,128)(2,1)} %get-tuple-element.45.activ, bf16[640,768]{1,0:T(8,128)(2,1)} %get-tuple-element.41.mixed_h.mixed, ...), custom_call_target="tpu_custom_call" | custom-call | tf_op jit(solution)/shard_map/tail/pallas_call | solution.py:1462
  224.6 0.0 copy-start.1
  224.6 1.7 slice_reduce_fusion
  226.2 0.7 slice.38
  227.0 1.5 fusion
  228.5 0.6 reshape.35
  229.1 0.0 copy-done
  229.1 0.0 copy-start.4
  229.1 0.0 copy-start.5
  229.1 0.0 copy-start.3
  229.1 0.9 copy.40
  230.1 0.0 copy-done.1
  230.1 0.0 copy-start.2
  230.1 0.9 copy.41
  231.0 0.0 copy-done.4
  231.0 0.7 copy.42
  231.7 0.0 copy-done.5
  231.7 0.6 copy.43
  232.4 0.0 copy-done.3
  232.4 0.8 copy.44
  233.2 0.0 copy-done.2
  233.2 0.8 copy.45
Async XLA Ops:
  169.9 59.3 %copy-start = (bf16[640,768]{1,0:T(8,128)(2,1)S(1)}, bf16[640,768]{1,0:T(8,128)(2,1)}, u32[]{:S(2)}) copy-start(bf16[640,768]{1,0:T(8,128)(2,1)} %get-tuple-element.81) | copy-start | bytes 2949124
  224.6 5.5 %copy-start.1 = (bf16[640,768]{1,0:T(8,128)(2,1)S(1)}, bf16[640,768]{1,0:T(8,128)(2,1)}, u32[]{:S(2)}) copy-start(bf16[640,768]{1,0:T(8,128)(2,1)} %get-tuple-element.82) | copy-start | bytes 2949124
  229.1 1.9 copy-start.4
  229.1 2.6 %copy-start.5 = (f32[24,768]{1,0:T(8,128)S(1)}, f32[24,768]{1,0:T(8,128)}, u32[]{:S(2)}) copy-start(f32[24,768]{1,0:T(8,128)} %get-tuple-element.87) | copy-start | bytes 221188
  229.1 3.2 %copy-start.3 = (f32[2,48,1536]{2,1,0:T(8,128)S(1)}, f32[2,48,1536]{2,1,0:T(8,128)}, u32[]{:S(2)}) copy-start(f32[2,48,1536]{2,1,0:T(8,128)} %get-tuple-element.93) | copy-start | bytes 1769476
  230.1 3.1 %copy-start.2 = (f32[2,48,1536]{2,1,0:T(8,128)S(1)}, f32[2,48,1536]{2,1,0:T(8,128)}, u32[]{:S(2)}) copy-start(f32[2,48,1536]{2,1,0:T(8,128)} %get-tuple-element.95) | copy-start | bytes 1769476
